TPU v7x, 256 devices: a whole 4x4x8 slice. The times are simulated.
256 devices in a mesh: seq: 32 (over x, z), head: 8 (over y, core).
Axes of the slice: x: 4, y: 4, z: 8, core: 2. Of those that a mesh axis runs over, the one named last changes fastest.
Arguments:
- queries: bfloat16 [32768, 4096], P('seq', 'head'), may hold values from -0.23925781 to 0.23925781
- keys: bfloat16 [32768, 4096], P('seq', 'head'), may hold values from -0.23925781 to 0.23925781
- values: bfloat16 [32768, 4096], P('seq', 'head'), may hold values from -1.5 to 1.5
- out_grad: bfloat16 [32768, 4096], P('seq', 'head'), may hold values from -1.5 to 1.5
- starts: int32 [32768], P('seq'), may hold values 0 or 1
- owners: int32 [32768, 1], P('seq'), may hold values from 0 to 7; in each aligned block of 1024 rows (0 to 1023, 1024 to 2047, ...) at most 256 rows name the same one
Outputs:
- returned: bfloat16 [65536, 3, 4096], P(('seq', 'head'))
Inputs may be any that keep to these rules, and one draw needn't show every extreme that they name: `owners`: among the 1024 tokens of one block, no owner is named by more than 256 tokens, a bound that some block reaches.
All inputs are finite; a program needn't handle non-finite values. No bound on the sum of `starts` on one device may be relied on, other than what follows from the above.
Results may differ from a plain program's by a relative error of at most 0.0049.
Values may be sent and summed in bfloat16 or wider, within the bound.
No kernel may reach another device: no remote copies, remote signals or barrier semaphores. Data moves between devices by JAX's collectives and lax.ppermute only.
A program may use at most 128 MiB of HBM per device.

v0:
```python
import jax
import jax.numpy as jnp
from jax import lax
from jax.sharding import PartitionSpec as P

HD = 128


def entering(part, axis, combine, identity, reverse):
    count = lax.axis_size(axis)
    place = lax.axis_index(axis)
    ahead = count - 1 - place if reverse else place
    gathered = jax.tree.map(lambda a: lax.all_gather(a, axis), part)
    state = jax.tree.map(lambda a, e: jnp.zeros_like(a) + jnp.asarray(e, a.dtype), part, identity)

    def one(turn, state):
        source = count - 1 - turn if reverse else turn
        return combine(
            state, jax.tree.map(lambda a: lax.dynamic_index_in_dim(a, source, 0, False), gathered)
        )

    return lax.fori_loop(0, ahead, one, state)


def chain_combine(earlier, later):
    return (earlier[0] * later[0], later[1] + later[0] * earlier[1])


def place_rows(block, owners, count):
    span = block.shape[0]
    owner_ids = owners[:, 0]
    onehot = (owner_ids[:, None] == lax.iota(jnp.int32, count)[None, :]).astype(jnp.int32)
    before = jnp.cumsum(onehot, axis=0, dtype=jnp.int32) - onehot
    slots = jnp.sum(before * onehot, axis=1)
    capacity = 2 * span // count
    target = owner_ids * capacity + slots
    buffer = jnp.zeros((count * capacity,) + block.shape[1:], block.dtype).at[target].set(block)
    return buffer.reshape((count, capacity) + block.shape[1:])


def shards(queries, keys, values, out_grad, starts, owners):
    span, feats = queries.shape
    heads = feats // HD
    head_shape = (span, heads, HD)
    query_h = queries.reshape(head_shape)
    key_h = keys.reshape(head_shape)
    value_h = values.reshape(head_shape)
    grad_h = out_grad.reshape(head_shape)
    segment = jnp.cumsum(starts, dtype=jnp.int32)
    position = lax.iota(jnp.int32, span)
    allowed = (position[None, :] <= position[:, None]) & (segment[:, None] == segment[None, :])
    first = (segment == 0).astype(jnp.bfloat16)[:, None, None]
    last = (segment == segment[-1]).astype(jnp.bfloat16)[:, None, None]
    keep = (segment[-1] == 0).astype(jnp.float32).reshape(1, 1, 1)
    fwd_local = jnp.einsum(
        "thd,the->hde", key_h * last, value_h, preferred_element_type=jnp.float32
    )
    bwd_local = jnp.einsum(
        "thd,the->hde", query_h * first, grad_h, preferred_element_type=jnp.float32
    )
    zeros = jnp.zeros((heads, HD, HD), jnp.float32)
    unity = jnp.ones((1, 1, 1), jnp.float32)
    fwd_in = entering((keep, fwd_local), "seq", chain_combine, (unity, zeros), False)[1]
    bwd_in = entering((keep, bwd_local), "seq", chain_combine, (unity, zeros), True)[1]
    score_ov = jnp.einsum("thd,shd->hts", grad_h, value_h, preferred_element_type=jnp.float32)
    weight_ov = jnp.where(allowed[None], score_ov, 0.0).astype(jnp.bfloat16)
    score_qk = jnp.einsum("thd,shd->hts", query_h, key_h, preferred_element_type=jnp.float32)
    weight_qk = jnp.where(allowed[None], score_qk, 0.0).astype(jnp.bfloat16)
    fwd_b = fwd_in.astype(jnp.bfloat16)
    bwd_b = bwd_in.astype(jnp.bfloat16)
    grad_q = jnp.einsum("hts,shd->thd", weight_ov, key_h, preferred_element_type=jnp.float32)
    grad_q = grad_q + first * jnp.einsum(
        "the,hde->thd", grad_h, fwd_b, preferred_element_type=jnp.float32
    )
    grad_q = grad_q.reshape(span, feats).astype(jnp.bfloat16)
    grad_k = jnp.einsum("hts,thd->shd", weight_ov, query_h, preferred_element_type=jnp.float32)
    grad_k = grad_k + last * jnp.einsum(
        "the,hde->thd", value_h, bwd_b, preferred_element_type=jnp.float32
    )
    grad_k = grad_k.reshape(span, feats).astype(jnp.bfloat16)
    grad_v = jnp.einsum("hts,thd->shd", weight_qk, grad_h, preferred_element_type=jnp.float32)
    grad_v = grad_v + last * jnp.einsum(
        "thd,hde->the", key_h, bwd_b, preferred_element_type=jnp.float32
    )
    grad_v = grad_v.reshape(span, feats).astype(jnp.bfloat16)
    count = lax.axis_size("head")
    stacked = jnp.stack([grad_q, grad_k, grad_v], axis=1)
    buffer = place_rows(stacked, owners, count)
    received = lax.all_to_all(buffer, "head", split_axis=0, concat_axis=3, tiled=True)
    return received[0]


def solution(mesh):
    in_specs = (
        P("seq", "head"),
        P("seq", "head"),
        P("seq", "head"),
        P("seq", "head"),
        P("seq"),
        P("seq", None),
    )
    out_specs = P(("seq", "head"), None, None)
    return jax.shard_map(shards, mesh=mesh, in_specs=in_specs, out_specs=out_specs, check_vma=False)
```

profile of v0, /device:TPU:230, one launch (start us, length us, event | category | flops | bytes accessed | tf_op | source)
XLA Modules:
  0.0 550.6 jit_solution(7866156423693164056)
XLA Ops:
  9.4 1.9 copy.83
  16.9 2.3 reduce-window.15
  20.9 69.9 %all-reduce = f32[32]{0:T(128)S(1)} all-reduce(f32[32]{0:T(128)S(1)} %dynamic-update-slice), channel_id=1, replica_groups=mesh['seq'=32,'head'=8] {'seq'}, use_global_device_ids=true, to_apply=%add | all-reduce | flops 32 | bytes 256
  91.6 2.7 select_convert_fusion.1
  94.3 3.2 copy-done.2
  97.5 4.3 fusion.29
  101.8 6.0 %all-gather.7.cloned.1.call-done = f32[128,128,128]{2,1,0:T(8,128)} async-done(((f32[4,128,128]{2,1,0:T(8,128)}), f32[128,128,128]{2,1,0:T(8,128)}) %all-gather.7.cloned.1.call-update) | async-done | bytes 8388624 | tf_op jit(solution)/shard_map/all_gather | solution.py:13
  107.9 1.8 fusion.5
  109.6 1.8 fusion.19
  111.4 94.3 %all-gather.5.cloned.1.call-done = f32[128,128,128]{2,1,0:T(8,128)} async-done(((f32[4,128,128]{2,1,0:T(8,128)}), f32[128,128,128]{2,1,0:T(8,128)}) %all-gather.5.cloned.1.call-update) | async-done | bytes 8388624 | tf_op jit(solution)/shard_map/all_gather | solution.py:13
  205.7 71.9 %while.26 = (s32[]{:T(128)}, f32[4,128,128]{2,1,0:T(8,128)S(1)}, s32[]{:T(128)}, f32[32,4,128,128]{3,2,1,0:T(8,128)}, f32[32,1,1,1]{0,3,2,1:T(1,128)S(1)}, /*index=5*/s32[]{:T(128)}, s32[]{:T(128)}, s32[]{:T(128)}) while((s32[]{:T(128)}, f32[4,128,128]{2,1,0:T(8,128)S(1)}, s32[]{:T(128)}, f32[32,4,128,128]{3,2,1,0:T(8,128)}, ...), condition=%wide.region_6.7_spmd, body=%wide.region_5.6_spmd.sunk | while | flops 131077 | bytes 786579 | solution.py:22
  206.4 1.7 bitcast_add_fusion.7
  208.7 1.7 bitcast_add_fusion.7
  211.0 1.7 bitcast_add_fusion.7
  213.3 1.7 bitcast_add_fusion.7
  215.6 1.7 bitcast_add_fusion.7
  217.9 1.7 bitcast_add_fusion.7
  220.3 1.7 bitcast_add_fusion.7
  222.6 1.7 bitcast_add_fusion.7
  224.9 1.7 bitcast_add_fusion.7
  231.8 1.7 bitcast_add_fusion.7
  234.1 1.7 bitcast_add_fusion.7
  236.5 1.7 bitcast_add_fusion.7
  238.8 1.7 bitcast_add_fusion.7
  245.7 1.7 bitcast_add_fusion.7
  248.0 1.7 bitcast_add_fusion.7
  250.3 1.7 bitcast_add_fusion.7
  252.7 1.7 bitcast_add_fusion.7
  255.0 1.7 bitcast_add_fusion.7
  259.6 1.7 bitcast_add_fusion.7
  261.9 1.7 bitcast_add_fusion.7
  264.2 1.7 bitcast_add_fusion.7
  266.6 1.7 bitcast_add_fusion.7
  268.9 1.7 bitcast_add_fusion.7
  275.8 1.7 bitcast_add_fusion.7
  277.7 7.4 %fusion.2 = bf16[1024,4,128]{0,2,1:T(8,128)(2,1)} fusion(f32[4,128,1024]{2,1,0:T(8,128)} %fusion.19, bf16[1024,4,128]{0,2,1:T(8,128)(2,1)S(1)} %bitcast.115, bf16[1024,4,128]{0,2,1:T(8,128)(2,1)} %bitcast.119, bf16[1024,4,128]{0,2,1:T(8,128)(2,1)S(1)} %bitcast.111, pred[1024,1024]{1,0:T(8,128)(4,1)} %copy-done.5, f32[1024]{0:T(1024)S(1)} %get-tuple-element.158), kind=kOutput, calls=%fused_computation.12 | convolution fusion | flops 2157445120 | bytes 7344128 | tf_op jit(solution)/shard_map/hts,thd->shd/dot_general | solution.py:81
  285.1 4.6 copy.75
  289.7 6.5 %fusion.3 = bf16[1024,4,128]{0,2,1:T(8,128)(2,1)} fusion(f32[4,128,1024]{2,1,0:T(8,128)} %fusion.5, bf16[1024,4,128]{0,2,1:T(8,128)(2,1)} %bitcast.120, bf16[4,1024,1024]{2,1,0:T(8,128)(2,1)} %copy-done.2, f32[1024]{0:T(1024)S(1)} %get-tuple-element.158), kind=kOutput, calls=%fused_computation.14 | convolution fusion | flops 1075314688 | bytes 12587008 | tf_op jit(solution)/shard_map/hts,thd->shd/dot_general | solution.py:76
  296.3 5.9 %copy.74 = bf16[1024,1,512]{2,1,0:T(2,128)(2,1)} copy(bf16[1024,1,512]{0,2,1:T(8,128)(2,1)} %bitcast.117) | data formatting | bytes 2097152 | tf_op jit(solution)/shard_map/convert_element_type | solution.py:80
  302.2 3.3 fusion.4
  305.5 6.0 %copy.73 = bf16[1024,1,512]{2,1,0:T(2,128)(2,1)} copy(bf16[1024,1,512]{0,2,1:T(8,128)(2,1)} %bitcast.112) | data formatting | bytes 2097152 | tf_op jit(solution)/shard_map/convert_element_type | solution.py:75
  311.5 9.4 %pad_maximum_fusion = bf16[1024,3,512]{2,1,0:T(4,128)(2,1)} fusion(bf16[1024,1,512]{2,1,0:T(2,128)(2,1)S(1)} %copy.75, bf16[1024,1,512]{2,1,0:T(2,128)(2,1)} %copy.74, bf16[1024,1,512]{2,1,0:T(2,128)(2,1)} %copy.73), kind=kLoop, calls=%fused_computation.7 | loop fusion | flops 9437184 | bytes 6291456 | tf_op jit(solution)/shard_map/stack | solution.py:87
  321.0 5.4 broadcast_in_dim.32
  326.4 117.5 %scatter_fusion = bf16[2048,3,512]{2,1,0:T(4,128)(2,1)} fusion(bf16[2048,3,512]{2,1,0:T(4,128)(2,1)} %broadcast_in_dim.32, s32[1024]{0:T(1024)S(1)} %bitcast.126, bf16[1024,3,512]{2,1,0:T(4,128)(2,1)} %pad_maximum_fusion), kind=kCustom, calls=%fused_computation | custom fusion | bytes 9441280 | tf_op jit(solution)/shard_map/scatter | solution.py:37
  443.8 5.2 copy.77
  449.0 77.4 %all_to_all.15 = bf16[8,256,3,512]{3,1,2,0:T(8,128)(2,1)} all-to-all(bf16[8,256,3,512]{3,1,2,0:T(8,128)(2,1)S(1)} %copy.77), channel_id=1, replica_groups=mesh['seq'=32,'head'=8] {'head'}, dimensions={0} | all-to-all | bytes 12582912 | tf_op jit(solution)/shard_map/all_to_all | solution.py:89
  526.4 8.7 %copy.78 = bf16[8,256,3,512]{1,3,0,2:T(8,128)(2,1)} copy(bf16[8,256,3,512]{3,1,2,0:T(8,128)(2,1)} %all_to_all.15) | data formatting | bytes 12582912 | tf_op jit(solution)/shard_map/all_to_all | solution.py:89
  535.1 8.7 %copy.79 = bf16[256,3,4096]{2,0,1:T(8,128)(2,1)} copy(bf16[256,3,4096]{0,2,1:T(8,128)(2,1)} %bitcast.107) | data formatting | bytes 12582912 | tf_op jit(solution)/shard_map/squeeze | solution.py:90
  (81 shorter events, 41.1 us)
Async XLA Ops:
  6.5 8.6 %copy-start = (bf16[1024,512]{1,0:T(8,128)(2,1)S(1)}, bf16[1024,512]{1,0:T(8,128)(2,1)}, u32[]{:S(2)}) copy-start(bf16[1024,512]{1,0:T(8,128)(2,1)} %param.12) | copy-start | bytes 3145732
  6.5 101.3 %all-gather.7.cloned.1.call-start = ((), (), s32[]{:S(2)}) async-start(), calls=%async_computation.2 | async-start | bytes 8650752 | tf_op jit(solution)/shard_map/all_gather | solution.py:13
  9.4 3.1 copy-start.4
  11.3 266.4 %copy-start.3 = (bf16[1024,512]{0,1:T(8,128)(2,1)}, bf16[1024,512]{0,1:T(8,128)(2,1)S(1)}, u32[]{:S(2)}) copy-start(bf16[1024,512]{0,1:T(8,128)(2,1)S(1)} %copy.83) | copy-start | bytes 3145732
  11.3 5.6 %copy-start.6 = (s32[1024,1]{0,1:T(1,128)S(1)}, s32[1024,1]{0,1:T(1,128)}, u32[]{:S(2)}) copy-start(s32[1024,1]{0,1:T(1,128)} %param.15) | copy-start | bytes 12292
  11.3 8.3 %copy-start.7 = (u32[256]{0:T(256)S(1)}, u32[256]{0:T(256)}, u32[]{:S(2)}) copy-start(u32[256]{0:T(256)} %constant.77) | copy-start | bytes 3076
  12.5 193.2 %all-gather.5.cloned.1.call-start = ((), (), s32[]{:S(2)}) async-start(), calls=%async_computation.1 | async-start | bytes 8650752 | tf_op jit(solution)/shard_map/all_gather | solution.py:13
  91.6 2.7 copy-start.5
  94.3 3.2 copy-start.2
  535.1 8.7 %copy-start.1 = (bf16[1024,512]{1,0:T(8,128)(2,1)S(1)}, bf16[1024,512]{1,0:T(8,128)(2,1)}, u32[]{:S(2)}) copy-start(bf16[1024,512]{1,0:T(8,128)(2,1)} %param.12) | copy-start | bytes 3145732
Sparse Core Ops, SparseCore 0:
  12.6 95.1 all-gather.6
  110.4 95.2 all-gather.4
where the time goes:
time: 556 us; the launch traced here: 551 us
  local copies, waits for them, and re-layouts  192 us (35%)
  blocking collectives  147 us (26%)
  waiting for transfers between devices  100 us (18%)
  other arithmetic  66.3 us (12%)
  matrix products  30.1 us (5%)
  between operations  14.2 us (3%)
    scatter x1, local copies, waits for them, and re-layouts, place_rows(): jnp.zeros((count * capacity,) + block.shape[1:], block.dtype).at[target]  117 us
    all_gather x2, waiting for transfers between devices, entering(): gathered = jax.tree.map(lambda a: lax.all_gather(a, axis), part)  100 us
    all_to_all x1, blocking collectives, shards(): lax.all_to_all(buffer, 'head', split_axis=0, concat_axis=3, tiled=True)  77.4 us
    unnamed x1, blocking collectives  69.9 us
    add x31, other arithmetic, chain_combine(): return (earlier[0] * later[0], later[1] + later[0] * earlier[1])  52 us
    dynamic_slice x31, local copies, waits for them, and re-layouts, one(): lax.dynamic_index_in_dim(a, source, 0, False)  19 us
  transfers between devices with their start and end apart: 2, of which 2 were waited for; matrix products, arithmetic and copies ran while one was open for 3% of the time, Pallas kernels for 0%

commit v1 on v0

v1 whole, which is shorter than its diff:
```python
import functools

import jax
import jax.numpy as jnp
from jax import lax
from jax.experimental import pallas as pl
from jax.experimental.pallas import tpu as pltpu
from jax.sharding import PartitionSpec as P

HD = 128
TILE = 256
F32 = jnp.float32
BF16 = jnp.bfloat16
VMEM_BYTES = 32 << 20


def dot_nn(a, b):
    return lax.dot_general(a, b, (((1,), (0,)), ((), ())), preferred_element_type=F32)


def dot_nt(a, b):
    return lax.dot_general(a, b, (((1,), (1,)), ((), ())), preferred_element_type=F32)


def dot_tn(a, b):
    return lax.dot_general(a, b, (((0,), (0,)), ((), ())), preferred_element_type=F32)


def params(steps=1):
    return pltpu.CompilerParams(
        dimension_semantics=("arbitrary",) * steps, vmem_limit_bytes=VMEM_BYTES
    )


def states_body(count, capacity, starts, owners, q, k, v, g, pay, seg_row, seg_col, dest):
    span = starts.shape[1]

    @pl.when(pl.program_id(0) == 0)
    def _():
        begin = starts[...]
        owner = owners[...]
        rows = lax.broadcasted_iota(jnp.int32, (count + 8, span), 0)
        hit = jnp.where(rows < count, owner, begin) == jnp.where(rows < count, rows, 1)
        before = (
            lax.broadcasted_iota(jnp.int32, (span, span), 1)
            <= lax.broadcasted_iota(jnp.int32, (span, span), 0)
        ).astype(F32).astype(BF16)
        sums = dot_nt(hit.astype(F32).astype(BF16), before)
        seg_row[...] = sums[count:]
        mine = owner == lax.broadcasted_iota(jnp.int32, (count, span), 0)
        slot = jnp.sum(jnp.where(mine, sums[:count] - 1.0, 0.0), axis=0, keepdims=True)
        dest[...] = owner * capacity + slot.astype(jnp.int32)
        wide = jnp.broadcast_to(begin, (HD, span)).astype(F32).astype(BF16)
        seg_col[...] = dot_nt(before, wide)

    segment = seg_col[...]
    total = segment[span - 1 :, :]
    first = (segment == 0.0).astype(F32).astype(BF16)
    last = (segment == total).astype(F32).astype(BF16)
    pieces = pay.shape[0]
    part = HD // pieces
    fwd = dot_tn(k[...] * last, v[...]).astype(BF16)
    bwd = dot_tn(q[...] * first, g[...]).astype(BF16)
    pay[:, :part, :] = fwd.reshape(pieces, part, HD)
    pay[:, part : 2 * part, :] = bwd.reshape(pieces, part, HD)
    keep = (total == 0.0).astype(F32)
    pay[:, 2 * part :, :] = jnp.broadcast_to(keep[None], (pieces, 16, HD)).astype(BF16)


def chain_body(count, part, got, out):
    fwd = jnp.zeros((part, HD), F32)
    bwd = jnp.zeros((part, HD), F32)
    for turn in range(count):
        out[turn, :part, :] = fwd.astype(BF16)
        keep = got[turn, 2 * part : 2 * part + 1, :].astype(F32)
        fwd = got[turn, :part, :].astype(F32) + keep * fwd
        back = count - 1 - turn
        out[back, part:, :] = bwd.astype(BF16)
        keep = got[back, 2 * part : 2 * part + 1, :].astype(F32)
        bwd = got[back, part : 2 * part, :].astype(F32) + keep * bwd


def local_body(seg_row, seg_col, q, k, v, g, out, mask, mask_t):
    span = q.shape[0]

    @pl.when(pl.program_id(0) == 0)
    def _():
        for lo in range(0, span, TILE):
            col = seg_col[lo : lo + TILE, :1]
            same = col == seg_row[:1, :]
            here = lo + lax.broadcasted_iota(jnp.int32, (TILE, span), 0)
            there = lax.broadcasted_iota(jnp.int32, (TILE, span), 1)
            mask[lo : lo + TILE, :] = (same & (there <= here)).astype(F32).astype(BF16)
            mask_t[lo : lo + TILE, :] = (same & (there >= here)).astype(F32).astype(BF16)

    for lo in range(0, span, TILE):
        hi = lo + TILE
        score = dot_nt(g[lo:hi, :], v[:hi, :]).astype(BF16) * mask[lo:hi, :hi]
        out[0, 0, lo:hi, :] = dot_nn(score, k[:hi, :])
        score = dot_nt(v[lo:hi, :], g[lo:, :]).astype(BF16) * mask_t[lo:hi, lo:]
        out[0, 1, lo:hi, :] = dot_nn(score, q[lo:, :])
        score = dot_nt(k[lo:hi, :], q[lo:, :]).astype(BF16) * mask_t[lo:hi, lo:]
        out[0, 2, lo:hi, :] = dot_nn(score, g[lo:, :])


def send_body(part, seg_col, dest, states, local, k, v, g, out, grads):
    span = k.shape[0]
    heads = local.shape[0]
    width = heads * HD
    capacity = out.shape[2]
    owner = pl.program_id(0)

    @pl.when(owner == 0)
    def _():
        segment = seg_col[...]
        first = (segment == 0.0).astype(F32)
        last = (segment == segment[span - 1 :, :]).astype(F32)
        pieces = HD // part
        for head in range(heads):
            own = slice(head * HD, (head + 1) * HD)
            rows = slice(head * pieces, (head + 1) * pieces)
            fwd = states[rows, :part, :].reshape(HD, HD)
            bwd = states[rows, part:, :].reshape(HD, HD)
            terms = (
                first * dot_nt(g[:, own], fwd),
                last * dot_nt(v[:, own], bwd),
                last * dot_nn(k[:, own], bwd),
            )
            for kind in range(3):
                at = kind * width + head * HD
                grads[:, at : at + HD] = (local[head, kind] + terms[kind]).astype(BF16)

    slots = owner * capacity + lax.broadcasted_iota(jnp.int32, (capacity, span), 0)
    pick = (dest[...] == slots).astype(F32).astype(BF16)
    rows = dot_nn(pick, grads[...]).astype(BF16)
    for kind in range(3):
        out[0, kind] = rows[:, kind * width : (kind + 1) * width]


def unpack_body(*refs):
    got, out = refs[0], refs[-1]
    out[...] = got[0]


def shards(chunks, queries, keys, values, out_grad, starts, owners):
    span, feats = queries.shape
    heads = feats // HD
    n_seq = lax.axis_size("seq")
    count = lax.axis_size("head")
    capacity = 2 * span // count
    part = heads * HD // n_seq
    pieces = HD // part
    full = lambda *shape: pl.BlockSpec(shape, lambda i: (0,) * len(shape))
    by_head = pl.BlockSpec((span, HD), lambda i: (0, i))
    starts_row = starts.reshape(1, span)
    owners_row = owners.reshape(1, span)

    payload, seg_row, seg_col, dest = pl.pallas_call(
        functools.partial(states_body, count, capacity),
        grid=(heads,),
        in_specs=[full(1, span), full(1, span)] + [by_head] * 4,
        out_specs=[
            pl.BlockSpec((pieces, 2 * part + 16, HD), lambda i: (i, 0, 0)),
            full(8, span),
            full(span, HD),
            full(1, span),
        ],
        out_shape=[
            jax.ShapeDtypeStruct((n_seq, 2 * part + 16, HD), BF16),
            jax.ShapeDtypeStruct((8, span), F32),
            jax.ShapeDtypeStruct((span, HD), F32),
            jax.ShapeDtypeStruct((1, span), jnp.int32),
        ],
        compiler_params=params(),
        name="states",
    )(starts_row, owners_row, queries, keys, values, out_grad)

    gathered = lax.all_to_all(payload, "seq", 0, 0, tiled=True)

    local = pl.pallas_call(
        local_body,
        grid=(heads,),
        in_specs=[full(8, span), full(span, HD)] + [by_head] * 4,
        out_specs=pl.BlockSpec((1, 3, span, HD), lambda i: (i, 0, 0, 0)),
        out_shape=jax.ShapeDtypeStruct((heads, 3, span, HD), F32),
        scratch_shapes=[pltpu.VMEM((span, span), BF16)] * 2,
        compiler_params=params(),
        cost_estimate=pl.CostEstimate(
            flops=heads * 8 * span * span * HD, bytes_accessed=10 << 20, transcendentals=0
        ),
        name="local",
    )(seg_row, seg_col, queries, keys, values, out_grad)

    chained = pl.pallas_call(
        functools.partial(chain_body, n_seq, part),
        out_shape=jax.ShapeDtypeStruct((n_seq, 2 * part, HD), BF16),
        compiler_params=params(0),
        name="chain",
    )(gathered)

    states = lax.all_to_all(chained, "seq", 0, 0, tiled=True)

    some = heads // chunks
    width = some * HD
    received = []
    for chunk in range(chunks):
        cols = pl.BlockSpec((span, width), lambda i, c=chunk: (0, c))
        buffer = pl.pallas_call(
            functools.partial(send_body, part),
            grid=(count,),
            in_specs=[
                full(span, HD),
                full(1, span),
                pl.BlockSpec((some * pieces, 2 * part, HD), lambda i, c=chunk: (c, 0, 0)),
                pl.BlockSpec((some, 3, span, HD), lambda i, c=chunk: (c, 0, 0, 0)),
                cols,
                cols,
                cols,
            ],
            out_specs=pl.BlockSpec((1, 3, capacity, width), lambda i: (i, 0, 0, 0)),
            out_shape=jax.ShapeDtypeStruct((count, 3, capacity, width), BF16),
            scratch_shapes=[pltpu.VMEM((span, 3 * width), BF16)],
            compiler_params=params(),
            cost_estimate=pl.CostEstimate(
                flops=2 * count * capacity * span * 3 * width,
                bytes_accessed=10 << 20,
                transcendentals=0,
            ),
            name="send",
        )(seg_col, dest, states, local, keys, values, out_grad)
        received.append(lax.all_to_all(buffer, "head", 0, 0, tiled=True))

    result = None
    for chunk in range(chunks):
        earlier = [] if result is None else [result]
        result = pl.pallas_call(
            unpack_body,
            grid=(count,),
            in_specs=[pl.BlockSpec((1, 3, capacity, width), lambda i: (i, 0, 0, 0))]
            + [pl.BlockSpec(memory_space=pl.ANY)] * len(earlier),
            out_specs=pl.BlockSpec(
                (3, capacity, width), lambda i, c=chunk: (0, 0, i * chunks + c)
            ),
            out_shape=jax.ShapeDtypeStruct((3, capacity, count * feats), BF16),
            input_output_aliases={1: 0} if earlier else {},
            compiler_params=params(),
            name="unpack",
        )(received[chunk], *earlier)
    return jnp.transpose(result, (1, 0, 2))


def solution(mesh):
    in_specs = (
        P("seq", "head"),
        P("seq", "head"),
        P("seq", "head"),
        P("seq", "head"),
        P("seq"),
        P("seq", None),
    )
    out_specs = P(("seq", "head"), None, None)
    return jax.shard_map(
        functools.partial(shards, 2),
        mesh=mesh,
        in_specs=in_specs,
        out_specs=out_specs,
        check_vma=False,
    )
```

time: 556 us -> 164 us (0.29)
  the two profiles are of different devices: /device:TPU:230 before, /device:TPU:1 now
where the time goes in v1:
time: 164 us; the launch traced here: 162 us
  waiting for transfers between devices  57.4 us (35%)
  Pallas kernels  35.7 us (22%)
  local copies, waits for them, and re-layouts  27.4 us (17%)
  blocking collectives  23.3 us (14%)
  starting transfers between devices  18.6 us (11%)
    all_to_all x2, waiting for transfers between devices, shards(): received.append(lax.all_to_all(buffer, 'head', 0, 0, tiled=True))  57.4 us
    unnamed x46, local copies, waits for them, and re-layouts  27.4 us
    all_to_all x1, blocking collectives, shards(): gathered = lax.all_to_all(payload, 'seq', 0, 0, tiled=True)  23.3 us
    pallas_call x1, Pallas kernels, shards(): pl.pallas_call(local_body, grid=(heads,), in_specs=[full(8, span), full(s...  12 us
    all_to_all x2, starting transfers between devices, shards(): received.append(lax.all_to_all(buffer, 'head', 0, 0, tiled=True))  11.1 us
    pallas_call x2, Pallas kernels, shards(): pl.pallas_call(functools.partial(send_body, part), grid=(count,), in_spec...  11 us
    pallas_call x2, Pallas kernels, shards(): pl.pallas_call(unpack_body, grid=(count,), in_specs=[pl.BlockSpec((1, 3,...  9.32 us
    all_to_all x1, starting transfers between devices, shards(): states = lax.all_to_all(chained, 'seq', 0, 0, tiled=True)  7.46 us
  transfers between devices with their start and end apart: 3, of which 2 were waited for; matrix products, arithmetic and copies ran while one was open for 0% of the time, Pallas kernels for 9%

profile of v1, /device:TPU:1, one launch (start us, length us, event | category | flops | bytes accessed | tf_op | source)
XLA Modules:
  0.0 162.5 jit_solution(13281043518475370079)
XLA Ops:
  0.0 0.0 copy-start.5
  0.0 1.2 copy-done.5
  1.2 0.0 copy-start.8
  1.2 1.2 copy-done.8
  2.5 0.0 copy-start.11
  2.5 1.2 copy-done.11
  3.7 0.0 copy-start.19
  3.7 1.2 copy-done.19
  4.9 0.0 copy-start.21
  4.9 0.7 copy-done.21
  5.6 0.7 copy-done.22
  6.3 3.3 %states.1 = (bf16[32,48,128]{2,1,0:T(8,128)(2,1)S(1)}, f32[8,1024]{1,0:T(8,128)S(1)}, f32[1024,128]{1,0:T(8,128)S(1)}, s32[1,1024]{1,0:T(1,128)S(1)}) custom-call(s32[1,1024]{1,0:T(1,128)S(1)} %bitcast.3, s32[1,1024]{1,0:T(1,128)S(1)} %bitcast.4, bf16[1024,512]{1,0:T(8,128)(2,1)S(1)} %copy-done.19, bf16[1024,512]{1,0:T(8,128)(2,1)S(1)} %copy-done.5, ...), custom_call_target="tpu_custom_call" | custom-call | tf_op jit(solution)/shard_map/states/pallas_call | solution.py:158
  9.6 0.0 copy-start.14
  9.6 0.8 copy-done.14
  10.4 23.3 %all_to_all.20.got = bf16[32,48,128]{2,1,0:T(8,128)(2,1)S(1)} all-to-all(bf16[32,48,128]{2,1,0:T(8,128)(2,1)S(1)} %get-tuple-element.11), channel_id=1, replica_groups=mesh['seq'=32,'head'=8] {'seq'}, dimensions={0} | all-to-all | bytes 786432 | tf_op jit(solution)/shard_map/all_to_all | solution.py:178
  33.7 0.1 chain.1
  33.8 0.0 copy-start.18
  33.8 0.7 copy-done.18
  34.5 7.5 %all-to-all-start.1 = ((bf16[32,32,128]{2,1,0:T(8,128)(2,1)}), bf16[32,32,128]{2,1,0:T(8,128)(2,1)S(1)}, u32[]{:S(2)}, u32[]{:S(2)}) async-start(bf16[32,32,128]{2,1,0:T(8,128)(2,1)} %copy-done.18), calls=%async_computation.1 | async-start | bytes 524288 | tf_op jit(solution)/shard_map/all_to_all | solution.py:201
  41.9 0.0 copy-done.6
  42.0 0.0 copy-done.9
  42.0 0.0 copy-done.12
  42.0 0.0 copy-start.15
  42.0 1.0 copy-done.15
  43.0 1.2 copy-done.20
  44.2 12.0 %local.1 = f32[4,3,1024,128]{3,2,1,0:T(8,128)S(1)} custom-call(f32[8,1024]{1,0:T(8,128)S(1)} %get-tuple-element.12.seg_row, f32[1024,128]{1,0:T(8,128)S(1)} %copy-done.15, bf16[1024,512]{1,0:T(8,128)(2,1)S(1)} %copy-done.20, bf16[1024,512]{1,0:T(8,128)(2,1)S(1)} %copy-done.6, bf16[1024,512]{1,0:T(8,128)(2,1)S(1)} %copy-done.9, bf16[1024,512]{1,0:T(8,128)(2,1)S(1)} %copy-done.12), custom_call_target="tpu_custom_call" | custom-call | flops 4294967296 | bytes 10485760 | tf_op jit(solution)/shard_map/local/pallas_call | solution.py:180
  56.2 0.0 copy-start
  56.2 2.7 %copy-done = f32[4,3,1024,128]{3,2,1,0:T(8,128)} copy-done((f32[4,3,1024,128]{3,2,1,0:T(8,128)}, f32[4,3,1024,128]{3,2,1,0:T(8,128)S(1)}, u32[]{:S(2)}) %copy-start) | copy-done | bytes 6291480
  58.9 0.0 all-to-all-done.1.states
  58.9 2.8 %copy-done.1 = f32[4,3,1024,128]{3,2,1,0:T(8,128)S(1)} copy-done((f32[4,3,1024,128]{3,2,1,0:T(8,128)S(1)}, f32[4,3,1024,128]{3,2,1,0:T(8,128)}, u32[]{:S(2)}) %copy-start.1) | copy-done | bytes 6291480
  61.7 1.0 copy-done.16
  62.8 5.5 %send.3 = bf16[8,3,256,256]{3,2,1,0:T(8,128)(2,1)S(1)} custom-call(f32[1024,128]{1,0:T(8,128)S(1)} %copy-done.16, s32[1,1024]{1,0:T(1,128)S(1)} %get-tuple-element.10.dest, bf16[32,32,128]{2,1,0:T(8,128)(2,1)S(1)} %all-to-all-done.1.states, f32[4,3,1024,128]{3,2,1,0:T(8,128)S(1)} %copy-done.1, bf16[1024,512]{1,0:T(8,128)(2,1)S(1)} %copy-done.6, ...), custom_call_target="tpu_custom_call" | custom-call | flops 3221225472 | bytes 10485760 | tf_op jit(solution)/shard_map/send/pallas_call | solution.py:208
  68.3 0.0 copy-start.4
  68.3 1.7 %copy-done.4 = bf16[8,3,256,256]{3,2,1,0:T(8,128)(2,1)} copy-done((bf16[8,3,256,256]{3,2,1,0:T(8,128)(2,1)}, bf16[8,3,256,256]{3,2,1,0:T(8,128)(2,1)S(1)}, u32[]{:S(2)}) %copy-start.4) | copy-done | bytes 3145752
  70.0 6.0 %all-to-all-start.3 = ((bf16[8,3,256,256]{3,2,1,0:T(8,128)(2,1)}), bf16[8,3,256,256]{3,2,1,0:T(8,128)(2,1)S(1)}, u32[]{:S(2)}, u32[]{:S(2)}) async-start(bf16[8,3,256,256]{3,2,1,0:T(8,128)(2,1)} %copy-done.4), calls=%async_computation.3 | async-start | bytes 6291456 | tf_op jit(solution)/shard_map/all_to_all | solution.py:231
  75.9 2.8 %copy-done.2 = f32[4,3,1024,128]{3,2,1,0:T(8,128)S(1)} copy-done((f32[4,3,1024,128]{3,2,1,0:T(8,128)S(1)}, f32[4,3,1024,128]{3,2,1,0:T(8,128)}, u32[]{:S(2)}) %copy-start.2) | copy-done | bytes 6291480
  78.7 1.2 copy-done.7
  79.9 1.2 copy-done.10
  81.2 1.2 copy-done.13
  82.4 1.0 copy-done.17
  83.4 5.5 %send.2 = bf16[8,3,256,256]{3,2,1,0:T(8,128)(2,1)S(1)} custom-call(f32[1024,128]{1,0:T(8,128)S(1)} %copy-done.17, s32[1,1024]{1,0:T(1,128)S(1)} %get-tuple-element.10.dest, bf16[32,32,128]{2,1,0:T(8,128)(2,1)S(1)} %all-to-all-done.1.states, f32[4,3,1024,128]{3,2,1,0:T(8,128)S(1)} %copy-done.2, bf16[1024,512]{1,0:T(8,128)(2,1)S(1)} %copy-done.7, ...), custom_call_target="tpu_custom_call" | custom-call | flops 3221225472 | bytes 10485760 | tf_op jit(solution)/shard_map/send/pallas_call | solution.py:208
  89.0 0.0 copy-start.3
  89.0 1.6 copy-done.3
  90.6 22.9 %all-to-all-done.3.refs_0_ = bf16[8,3,256,256]{3,2,1,0:T(8,128)(2,1)S(1)} async-done(((bf16[8,3,256,256]{3,2,1,0:T(8,128)(2,1)}), bf16[8,3,256,256]{3,2,1,0:T(8,128)(2,1)S(1)}, u32[]{:S(2)}, u32[]{:S(2)}) %all-to-all-start.3) | async-done | bytes 3145760 | tf_op jit(solution)/shard_map/all_to_all | solution.py:231
  113.5 5.2 %all-to-all-start.2 = ((bf16[8,3,256,256]{3,2,1,0:T(8,128)(2,1)}), bf16[8,3,256,256]{3,2,1,0:T(8,128)(2,1)}, u32[]{:S(2)}, u32[]{:S(2)}) async-start(bf16[8,3,256,256]{3,2,1,0:T(8,128)(2,1)} %copy-done.3), calls=%async_computation.2 | async-start | bytes 6291456 | tf_op jit(solution)/shard_map/all_to_all | solution.py:231
  118.7 3.2 %unpack.2.refs_1_ = bf16[3,256,4096]{2,1,0:T(8,128)(2,1)} custom-call(bf16[8,3,256,256]{3,2,1,0:T(8,128)(2,1)S(1)} %all-to-all-done.3.refs_0_), custom_call_target="tpu_custom_call" | custom-call | tf_op jit(solution)/shard_map/unpack/pallas_call | solution.py:236
  121.9 34.5 %all-to-all-done.2.refs_0_ = bf16[8,3,256,256]{3,2,1,0:T(8,128)(2,1)} async-done(((bf16[8,3,256,256]{3,2,1,0:T(8,128)(2,1)}), bf16[8,3,256,256]{3,2,1,0:T(8,128)(2,1)}, u32[]{:S(2)}, u32[]{:S(2)}) %all-to-all-start.2) | async-done | bytes 3145760 | tf_op jit(solution)/shard_map/all_to_all | solution.py:231
  156.4 6.1 %unpack.3 = bf16[3,256,4096]{2,1,0:T(8,128)(2,1)} custom-call(bf16[8,3,256,256]{3,2,1,0:T(8,128)(2,1)} %all-to-all-done.2.refs_0_, bf16[3,256,4096]{2,1,0:T(8,128)(2,1)} %unpack.2.refs_1_), custom_call_target="tpu_custom_call", output_to_operand_aliasing={{}: (1, {})} | custom-call | tf_op jit(solution)/shard_map/unpack/pallas_call | solution.py:236
  (12 shorter events, 0.0 us)
Async XLA Ops:
  0.0 1.2 copy-start.5
  1.2 1.2 copy-start.8
  2.5 1.2 copy-start.11
  3.7 1.2 copy-start.19
  4.9 0.7 copy-start.21
  5.6 0.7 copy-start.22
  6.3 35.7 %copy-start.6 = (bf16[1024,512]{1,0:T(8,128)(2,1)S(1)}, bf16[1024,512]{1,0:T(8,128)(2,1)}, u32[]{:S(2)}) copy-start(bf16[1024,512]{1,0:T(8,128)(2,1)} %k.7) | copy-start | bytes 3145732
  6.3 35.7 %copy-start.9 = (bf16[1024,512]{1,0:T(8,128)(2,1)S(1)}, bf16[1024,512]{1,0:T(8,128)(2,1)}, u32[]{:S(2)}) copy-start(bf16[1024,512]{1,0:T(8,128)(2,1)} %v.7) | copy-start | bytes 3145732
  6.3 35.7 %copy-start.12 = (bf16[1024,512]{1,0:T(8,128)(2,1)S(1)}, bf16[1024,512]{1,0:T(8,128)(2,1)}, u32[]{:S(2)}) copy-start(bf16[1024,512]{1,0:T(8,128)(2,1)} %g.7) | copy-start | bytes 3145732
  9.6 0.8 copy-start.14
  33.8 0.7 copy-start.18
  34.5 24.5 %all-to-all-start.1 = ((bf16[32,32,128]{2,1,0:T(8,128)(2,1)}), bf16[32,32,128]{2,1,0:T(8,128)(2,1)S(1)}, u32[]{:S(2)}, u32[]{:S(2)}) async-start(bf16[32,32,128]{2,1,0:T(8,128)(2,1)} %copy-done.18), calls=%async_computation.1 | async-start | bytes 524288 | tf_op jit(solution)/shard_map/all_to_all | solution.py:201
  42.0 1.0 copy-start.15
  43.0 1.2 copy-start.20
  56.2 2.7 %copy-start = (f32[4,3,1024,128]{3,2,1,0:T(8,128)}, f32[4,3,1024,128]{3,2,1,0:T(8,128)S(1)}, u32[]{:S(2)}) copy-start(f32[4,3,1024,128]{3,2,1,0:T(8,128)S(1)} %local.1) | copy-start | bytes 18874372
  58.9 2.8 %copy-start.1 = (f32[4,3,1024,128]{3,2,1,0:T(8,128)S(1)}, f32[4,3,1024,128]{3,2,1,0:T(8,128)}, u32[]{:S(2)}) copy-start(f32[4,3,1024,128]{3,2,1,0:T(8,128)} %copy-done) | copy-start | bytes 18874372
  61.7 1.0 copy-start.16
  68.3 1.7 %copy-start.4 = (bf16[8,3,256,256]{3,2,1,0:T(8,128)(2,1)}, bf16[8,3,256,256]{3,2,1,0:T(8,128)(2,1)S(1)}, u32[]{:S(2)}) copy-start(bf16[8,3,256,256]{3,2,1,0:T(8,128)(2,1)S(1)} %send.3) | copy-start | bytes 9437188
  70.0 43.5 %all-to-all-start.3 = ((bf16[8,3,256,256]{3,2,1,0:T(8,128)(2,1)}), bf16[8,3,256,256]{3,2,1,0:T(8,128)(2,1)S(1)}, u32[]{:S(2)}, u32[]{:S(2)}) async-start(bf16[8,3,256,256]{3,2,1,0:T(8,128)(2,1)} %copy-done.4), calls=%async_computation.3 | async-start | bytes 6291456 | tf_op jit(solution)/shard_map/all_to_all | solution.py:231
  75.9 2.8 %copy-start.2 = (f32[4,3,1024,128]{3,2,1,0:T(8,128)S(1)}, f32[4,3,1024,128]{3,2,1,0:T(8,128)}, u32[]{:S(2)}) copy-start(f32[4,3,1024,128]{3,2,1,0:T(8,128)} %copy-done) | copy-start | bytes 18874372
  78.7 1.2 copy-start.7
  79.9 1.2 copy-start.10
  81.2 1.2 copy-start.13
  82.4 1.0 copy-start.17
  89.0 1.6 %copy-start.3 = (bf16[8,3,256,256]{3,2,1,0:T(8,128)(2,1)}, bf16[8,3,256,256]{3,2,1,0:T(8,128)(2,1)S(1)}, u32[]{:S(2)}) copy-start(bf16[8,3,256,256]{3,2,1,0:T(8,128)(2,1)S(1)} %send.2) | copy-start | bytes 9437188
  113.5 42.9 %all-to-all-start.2 = ((bf16[8,3,256,256]{3,2,1,0:T(8,128)(2,1)}), bf16[8,3,256,256]{3,2,1,0:T(8,128)(2,1)}, u32[]{:S(2)}, u32[]{:S(2)}) async-start(bf16[8,3,256,256]{3,2,1,0:T(8,128)(2,1)} %copy-done.3), calls=%async_computation.2 | async-start | bytes 6291456 | tf_op jit(solution)/shard_map/all_to_all | solution.py:231

commit v2 on v1

v2 whole, which is shorter than its diff:
```python
import functools

import jax
import jax.numpy as jnp
from jax import lax
from jax.experimental import pallas as pl
from jax.experimental.pallas import tpu as pltpu
from jax.sharding import PartitionSpec as P

HD = 128
TILE = 256
F32 = jnp.float32
BF16 = jnp.bfloat16


def dot_nn(a, b):
    return lax.dot_general(a, b, (((1,), (0,)), ((), ())), preferred_element_type=F32)


def dot_nt(a, b):
    return lax.dot_general(a, b, (((1,), (1,)), ((), ())), preferred_element_type=F32)


def dot_tn(a, b):
    return lax.dot_general(a, b, (((0,), (0,)), ((), ())), preferred_element_type=F32)


def params(steps=1, mebibytes=24):
    return pltpu.CompilerParams(
        dimension_semantics=("arbitrary",) * steps, vmem_limit_bytes=mebibytes << 20
    )


def states_body(count, capacity, starts, owners, q, k, v, g, pay, seg_row, seg_col, dest):
    span = starts.shape[1]

    @pl.when(pl.program_id(0) == 0)
    def _():
        begin = starts[...]
        owner = owners[...]
        rows = lax.broadcasted_iota(jnp.int32, (count + 8, span), 0)
        hit = jnp.where(rows < count, owner, begin) == jnp.where(rows < count, rows, 1)
        hit = hit.astype(F32)
        lanes = range(0, span, HD)
        stack = jnp.concatenate([hit[:, at : at + HD] for at in lanes], axis=0).astype(BF16)
        before = (
            lax.broadcasted_iota(jnp.int32, (HD, HD), 0)
            <= lax.broadcasted_iota(jnp.int32, (HD, HD), 1)
        ).astype(F32).astype(BF16)
        inner = dot_nn(stack, before)
        whole = dot_nn(stack, jnp.ones((HD, HD), BF16))
        offset = jnp.zeros((count + 8, HD), F32)
        for turn, at in enumerate(lanes):
            mine = slice(turn * (count + 8), (turn + 1) * (count + 8))
            sums = inner[mine] + offset
            offset = offset + whole[mine]
            seg_row[:, at : at + HD] = sums[count:]
            slot = jnp.sum(
                hit[:count, at : at + HD] * (sums[:count] - 1.0), axis=0, keepdims=True
            )
            dest[:, at : at + HD] = owner[:, at : at + HD] * capacity + slot.astype(jnp.int32)
            seg_col[at : at + HD, :] = jnp.broadcast_to(sums[count : count + 1], (HD, HD)).T

    segment = seg_col[...]
    total = segment[span - 1 :, :]
    first = (segment == 0.0).astype(F32).astype(BF16)
    last = (segment == total).astype(F32).astype(BF16)
    pieces = pay.shape[0]
    part = HD // pieces
    fwd = dot_tn(k[...] * last, v[...]).astype(BF16)
    bwd = dot_tn(q[...] * first, g[...]).astype(BF16)
    pay[:, :part, :] = fwd.reshape(pieces, part, HD)
    pay[:, part : 2 * part, :] = bwd.reshape(pieces, part, HD)
    keep = (total == 0.0).astype(F32)
    pay[:, 2 * part :, :] = jnp.broadcast_to(keep[None], (pieces, 16, HD)).astype(BF16)


def chain_body(count, part, got, after, out):
    del after
    fwd = jnp.zeros((part, HD), F32)
    bwd = jnp.zeros((part, HD), F32)
    for turn in range(count):
        out[turn, :part, :] = fwd.astype(BF16)
        keep = got[turn, 2 * part : 2 * part + 1, :].astype(F32)
        fwd = got[turn, :part, :].astype(F32) + keep * fwd
        back = count - 1 - turn
        out[back, part:, :] = bwd.astype(BF16)
        keep = got[back, 2 * part : 2 * part + 1, :].astype(F32)
        bwd = got[back, part : 2 * part, :].astype(F32) + keep * bwd


def local_body(seg_row, seg_col, q, k, v, g, out, token, mask, mask_t):
    span = q.shape[0]
    token[...] = jnp.zeros_like(token)

    @pl.when(pl.program_id(0) == 0)
    def _():
        for lo in range(0, span, TILE):
            col = seg_col[lo : lo + TILE, :1]
            same = col == seg_row[:1, :]
            here = lo + lax.broadcasted_iota(jnp.int32, (TILE, span), 0)
            there = lax.broadcasted_iota(jnp.int32, (TILE, span), 1)
            mask[lo : lo + TILE, :] = (same & (there <= here)).astype(F32).astype(BF16)
            mask_t[lo : lo + TILE, :] = (same & (there >= here)).astype(F32).astype(BF16)

    for lo in range(0, span, TILE):
        hi = lo + TILE
        score = dot_nt(g[lo:hi, :], v[:hi, :]).astype(BF16) * mask[lo:hi, :hi]
        out[0, 0, lo:hi, :] = dot_nn(score, k[:hi, :])
        score = dot_nt(v[lo:hi, :], g[lo:, :]).astype(BF16) * mask_t[lo:hi, lo:]
        out[0, 1, lo:hi, :] = dot_nn(score, q[lo:, :])
        score = dot_nt(k[lo:hi, :], q[lo:, :]).astype(BF16) * mask_t[lo:hi, lo:]
        out[0, 2, lo:hi, :] = dot_nn(score, g[lo:, :])


def pick_rows(dest, owner, capacity):
    shape = (capacity, dest.shape[1])
    slots = owner * capacity + lax.broadcasted_iota(jnp.int32, shape, 0)
    return (dest[...] == slots).astype(F32).astype(BF16)


def edges(seg_col):
    segment = seg_col[...]
    first = (segment == 0.0).astype(F32)
    last = (segment == segment[segment.shape[0] - 1 :, :]).astype(F32)
    return first, last


def ahead_body(targets, seg_col, dest, local, k, v, g, kept, raw, pick):
    many, _, capacity, _ = kept.shape
    head = pl.program_id(0)

    @pl.when(head == 0)
    def _():
        for turn in range(many):
            pick[turn] = pick_rows(dest, targets[turn], capacity)

    first, last = edges(seg_col)
    first, last = first.astype(BF16), last.astype(BF16)
    exact = [local[0, kind] for kind in range(3)]
    high = [part.astype(BF16) for part in exact]
    low = [(part - near.astype(F32)).astype(BF16) for part, near in zip(exact, high)]
    rows = [g[...] * first, v[...] * last, k[...] * last]
    stack = jnp.concatenate(high + low + rows, axis=1)
    for turn in range(many):
        moved = dot_nn(pick[turn], stack)
        for kind in range(3):
            at = kind * HD
            kept[turn, kind] = moved[:, at : at + HD] + moved[:, 3 * HD + at : 4 * HD + at]
            raw[turn, kind] = moved[:, 6 * HD + at : 7 * HD + at].astype(BF16)


def terms_of(states, head, part, g, v, k):
    pieces = HD // part
    rows = slice(head * pieces, (head + 1) * pieces)
    fwd = states[rows, :part, :].reshape(HD, HD)
    bwd = states[rows, part:, :].reshape(HD, HD)
    return dot_nt(g, fwd), dot_nt(v, bwd), dot_nn(k, bwd)


def finish_body(part, kept_q, kept_k, kept_v, raw_q, raw_k, raw_v, states, out):
    for head in range(out.shape[2] // HD):
        own = slice(head * HD, (head + 1) * HD)
        rows = [raw[0, 0, :, own] for raw in (raw_q, raw_k, raw_v)]
        terms = terms_of(states, head, part, *rows)
        for kind, kept in enumerate((kept_q, kept_k, kept_v)):
            out[kind, :, own] = (kept[0, 0, :, own] + terms[kind]).astype(BF16)


def combine_body(part, seg_col, states, local, k, v, g, grads):
    first, last = edges(seg_col)
    terms = terms_of(states, 0, part, g[...], v[...], k[...])
    own = pl.ds(pl.multiple_of(pl.program_id(0) * HD, HD), HD)
    for kind, edge in enumerate((first, last, last)):
        grads[kind, :, own] = (local[0, kind] + edge * terms[kind]).astype(BF16)


def place_body(target, dest, grads, out):
    pick = pick_rows(dest, target[0], out.shape[1])
    for kind in range(3):
        out[kind] = dot_nn(pick, grads[kind]).astype(BF16)


def unpack_body(many, sources, *refs):
    out, held, sems, out_sems = refs[-4:]
    feats = refs[0].shape[2]
    loads = [
        pltpu.make_async_copy(refs[turn], held.at[turn], sems.at[turn]) for turn in range(many)
    ]
    for load in loads:
        load.start()
    stores = []
    for turn in range(many):
        loads[turn].wait()
        cols = pl.ds(pl.multiple_of(sources[turn] * feats, feats), feats)
        store = pltpu.make_async_copy(
            held.at[turn], out.at[:, :, cols], out_sems.at[turn]
        )
        store.start()
        stores.append(store)
    for store in stores:
        store.wait()


def shards(queries, keys, values, out_grad, starts, owners):
    span, feats = queries.shape
    heads = feats // HD
    n_seq = lax.axis_size("seq")
    count = lax.axis_size("head")
    capacity = 2 * span // count
    part = heads * HD // n_seq
    pieces = HD // part
    full = lambda *shape: pl.BlockSpec(shape, lambda i: (0,) * len(shape))
    by_head = pl.BlockSpec((span, HD), lambda i: (0, i))
    whole = pl.BlockSpec(memory_space=pltpu.VMEM)
    smem = pl.BlockSpec(memory_space=pltpu.SMEM)
    hbm = lambda array: pltpu.with_memory_space_constraint(array, pltpu.HBM)
    in_hbm = [hbm(array) for array in (queries, keys, values, out_grad)]
    starts_row = starts.reshape(1, span)
    owners_row = owners.reshape(1, span)

    payload, seg_row, seg_col, dest = pl.pallas_call(
        functools.partial(states_body, count, capacity),
        grid=(heads,),
        in_specs=[full(1, span), full(1, span)] + [by_head] * 4,
        out_specs=[
            pl.BlockSpec((pieces, 2 * part + 16, HD), lambda i: (i, 0, 0)),
            full(8, span),
            full(span, HD),
            full(1, span),
        ],
        out_shape=[
            jax.ShapeDtypeStruct((n_seq, 2 * part + 16, HD), BF16),
            jax.ShapeDtypeStruct((8, span), F32),
            jax.ShapeDtypeStruct((span, HD), F32),
            jax.ShapeDtypeStruct((1, span), jnp.int32),
        ],
        compiler_params=params(1, 60),
        name="states",
    )(starts_row, owners_row, *in_hbm)

    gathered = lax.all_to_all(payload, "seq", 0, 0, tiled=True)

    local, token = pl.pallas_call(
        local_body,
        grid=(heads,),
        in_specs=[full(8, span), full(span, HD)] + [by_head] * 4,
        out_specs=[pl.BlockSpec((1, 3, span, HD), lambda i: (i, 0, 0, 0)), full(8, HD)],
        out_shape=[
            pltpu.HBM((heads, 3, span, HD), F32),
            jax.ShapeDtypeStruct((8, HD), F32),
        ],
        scratch_shapes=[pltpu.VMEM((span, span), BF16)] * 2,
        compiler_params=params(),
        cost_estimate=pl.CostEstimate(
            flops=heads * 8 * span * span * HD, bytes_accessed=10 << 20, transcendentals=0
        ),
        name="local",
    )(seg_row, hbm(seg_col), *in_hbm)

    chained = pl.pallas_call(
        functools.partial(chain_body, n_seq, part),
        in_specs=[whole] * 2,
        out_specs=whole,
        out_shape=jax.ShapeDtypeStruct((n_seq, 2 * part, HD), BF16),
        compiler_params=params(0),
        name="chain",
    )(gathered, token)

    states = lax.all_to_all(chained, "seq", 0, 0, tiled=True)

    me = lax.axis_index("head")
    rows = count // 2
    hops = [(rows // 2, 0), (rows // 2, 1)]
    far = len(hops)
    for step in range(1, rows // 2):
        hops += [(step, 0), (rows - step, 0), (step, 1), (rows - step, 1)]
    hops += [(0, 1), (0, 0)]

    def moved(index, hop, sign):
        row = (index // 2 + sign * hop[0]) % rows
        return row * 2 + (index % 2 + hop[1]) % 2

    def scalars(*indices):
        return jnp.stack([index.astype(jnp.int32) for index in indices])

    fixed = lambda *shape: pl.BlockSpec(shape, lambda i, *t: (0,) * len(shape))
    local_block = pl.BlockSpec((1, 3, span, HD), lambda i, *t: (i, 0, 0, 0))
    raw_block = pl.BlockSpec((span, HD), lambda i, *t: (0, i))
    out_block = pl.BlockSpec((far, 3, capacity, HD), lambda i, *t: (0, 0, 0, i))
    kept, raw = pl.pallas_call(
        ahead_body,
        grid_spec=pltpu.PrefetchScalarGridSpec(
            num_scalar_prefetch=1,
            grid=(heads,),
            in_specs=[fixed(span, HD), fixed(1, span), local_block] + [raw_block] * 3,
            out_specs=[out_block, out_block],
            scratch_shapes=[pltpu.VMEM((far, capacity, span), BF16)],
        ),
        out_shape=[
            pltpu.HBM((far, 3, capacity, feats), F32),
            pltpu.HBM((far, 3, capacity, feats), BF16),
        ],
        compiler_params=params(1),
        cost_estimate=pl.CostEstimate(
            flops=2 * far * capacity * span * 9 * feats, bytes_accessed=1 << 20, transcendentals=0
        ),
        name="ahead",
    )(
        scalars(*[moved(me, hop, 1) for hop in hops[:far]]),
        hbm(seg_col),
        hbm(dest),
        hbm(local),
        *in_hbm[1:],
    )

    def finish(turn):
        blocks = [
            pl.BlockSpec((1, 1, capacity, feats), lambda i, n=turn, kind=kind: (n, kind, 0, 0))
            for kind in range(3)
        ]
        return pl.pallas_call(
            functools.partial(finish_body, part),
            grid=(1,),
            in_specs=blocks * 2 + [whole],
            out_specs=whole,
            out_shape=pltpu.VMEM((3, capacity, feats), BF16),
            compiler_params=params(),
            cost_estimate=pl.CostEstimate(
                flops=6 * capacity * feats * HD, bytes_accessed=1 << 20, transcendentals=0
            ),
            name="finish",
        )(*[hbm(kept)] * 3, *[hbm(raw)] * 3, states)

    def combine():
        return pl.pallas_call(
            functools.partial(combine_body, part),
            grid=(heads,),
            in_specs=[
                fixed(span, HD),
                pl.BlockSpec((pieces, 2 * part, HD), lambda i: (i, 0, 0)),
                local_block,
            ]
            + [raw_block] * 3,
            out_specs=whole,
            out_shape=pltpu.VMEM((3, span, feats), BF16),
            compiler_params=params(1),
            cost_estimate=pl.CostEstimate(
                flops=6 * span * feats * HD, bytes_accessed=1 << 20, transcendentals=0
            ),
            name="combine",
        )(hbm(seg_col), states, hbm(local), *in_hbm[1:])

    def place(hop, grads):
        cost = pl.CostEstimate(
            flops=2 * capacity * span * 3 * feats, bytes_accessed=1 << 20, transcendentals=0
        )
        target = scalars(moved(me, hop, 1))
        if hop == (0, 0):
            return pl.pallas_call(
                place_body,
                grid_spec=pltpu.PrefetchScalarGridSpec(
                    num_scalar_prefetch=1,
                    grid=(1,),
                    in_specs=[whole, whole],
                    out_specs=pl.BlockSpec((3, capacity, feats), lambda i, t: (0, 0, t[0])),
                ),
                out_shape=jax.ShapeDtypeStruct((3, capacity, count * feats), BF16),
                compiler_params=params(),
                cost_estimate=cost,
                name="place",
            )(target, dest, grads)
        return pl.pallas_call(
            place_body,
            in_specs=[smem, whole, whole],
            out_specs=whole,
            out_shape=pltpu.VMEM((3, capacity, feats), BF16),
            compiler_params=params(0),
            cost_estimate=cost,
            name="place",
        )(target, dest, grads)

    def sent(chunk, hop):
        return lax.ppermute(
            chunk, "head", [(index, moved(index, hop, 1)) for index in range(count)]
        )

    received = [sent(finish(turn), hop) for turn, hop in enumerate(hops[:far])]
    grads = combine()
    received += [sent(place(hop, grads), hop) for hop in hops[far:-1]]
    result = place(hops[-1], grads)
    for lo, hi in ((0, far), (far, count - 1)):
        many = hi - lo
        result = pl.pallas_call(
            functools.partial(unpack_body, many),
            in_specs=[smem] + [pl.BlockSpec(memory_space=pl.ANY)] * (many + 1),
            out_specs=pl.BlockSpec(memory_space=pl.ANY),
            out_shape=jax.ShapeDtypeStruct((3, capacity, count * feats), BF16),
            scratch_shapes=[
                pltpu.VMEM((many, 3, capacity, feats), BF16),
                pltpu.SemaphoreType.DMA((many,)),
                pltpu.SemaphoreType.DMA((many,)),
            ],
            input_output_aliases={many + 1: 0},
            compiler_params=params(0, 16),
            cost_estimate=pl.CostEstimate(flops=0, bytes_accessed=1 << 20, transcendentals=0),
            name="unpack",
        )(
            scalars(*[moved(me, hop, -1) for hop in hops[lo:hi]]),
            *[hbm(one) for one in received[lo:hi]],
            result,
        )
    return jnp.transpose(result, (1, 0, 2))


def solution(mesh):
    in_specs = (
        P("seq", "head"),
        P("seq", "head"),
        P("seq", "head"),
        P("seq", "head"),
        P("seq"),
        P("seq", None),
    )
    out_specs = P(("seq", "head"), None, None)
    return jax.shard_map(
        shards,
        mesh=mesh,
        in_specs=in_specs,
        out_specs=out_specs,
        check_vma=False,
    )
```

time: 164 us -> 134 us (0.82)
  local copies, waits for them, and re-layouts: 27.4 us -> 0.84 us
  blocking collectives: 23.3 us -> 0 us
  Pallas kernels: 35.7 us -> 58.9 us
  waiting for transfers between devices: 57.4 us -> 40.6 us
  starting transfers between devices: 18.6 us -> 32.4 us
    all_to_all x2 -> x1, waiting for transfers between devices: 57.4 us -> 0.01 us  [shards(): gathered = lax.all_to_all(payload, 'seq', 0, 0, tiled=True)]
    ppermute x0 -> x7, waiting for transfers between devices: none -> 40.6 us  [sent(): lax.ppermute(chunk, 'head', [(index, moved(index, hop, 1)) for index in r...]
    unnamed x46 -> x4, local copies, waits for them, and re-layouts: 27.4 us -> 0.76 us
    all_to_all x1 -> x0, blocking collectives: 23.3 us -> none  [shards(): gathered = lax.all_to_all(payload, 'seq', 0, 0, tiled=True)]
    pallas_call x5 -> x13, Pallas kernels: 20.4 us -> 40.2 us  [the longest x1 10.7 us: shards(): pl.pallas_call(ahead_body, grid_spec=pltpu.PrefetchScalarGridSpec(num_sca...]
    ppermute x0 -> x7, starting transfers between devices: none -> 11.3 us  [sent(): lax.ppermute(chunk, 'head', [(index, moved(index, hop, 1)) for index in r...]
    pallas_call x1, Pallas kernels: 12 us -> 13.9 us  [shards(): pl.pallas_call(local_body, grid=(heads,), in_specs=[full(8, span), full(s...]
    all_to_all x1, starting transfers between devices: 7.46 us -> 9.22 us  [shards(): states = lax.all_to_all(chained, 'seq', 0, 0, tiled=True)]
  transfers between devices with their start and end apart: 3 -> 9, of which waited for: 2 -> 4; matrix products, arithmetic and copies ran while one was open for 0% -> 0% of each run, Pallas kernels for 9% -> 35%
where the time goes in v2:
time: 134 us; the launch traced here: 133 us
  Pallas kernels  58.9 us (44%)
  waiting for transfers between devices  40.6 us (30%)
  starting transfers between devices  32.4 us (24%)
    ppermute x7, waiting for transfers between devices, sent(): lax.ppermute(chunk, 'head', [(index, moved(index, hop, 1)) for index in r...  40.6 us
    pallas_call x1, Pallas kernels, shards(): pl.pallas_call(local_body, grid=(heads,), in_specs=[full(8, span), full(s...  13.9 us
    all_to_all x1, starting transfers between devices, shards(): gathered = lax.all_to_all(payload, 'seq', 0, 0, tiled=True)  11.9 us
    ppermute x7, starting transfers between devices, sent(): lax.ppermute(chunk, 'head', [(index, moved(index, hop, 1)) for index in r...  11.3 us
    pallas_call x1, Pallas kernels, shards(): pl.pallas_call(ahead_body, grid_spec=pltpu.PrefetchScalarGridSpec(num_sca...  10.7 us
    pallas_call x5, Pallas kernels, place(): pl.pallas_call(place_body, in_specs=[smem, whole, whole], out_specs=whole...  9.39 us
    all_to_all x1, starting transfers between devices, shards(): states = lax.all_to_all(chained, 'seq', 0, 0, tiled=True)  9.22 us
    pallas_call x2, Pallas kernels, shards(): pl.pallas_call(functools.partial(unpack_body, many), in_specs=[smem] + [p...  6.52 us
  transfers between devices with their start and end apart: 9, of which 4 were waited for; matrix products, arithmetic and copies ran while one was open for 0% of the time, Pallas kernels for 35%

profile of v2, /device:TPU:1, one launch (start us, length us, event | category | flops | bytes accessed | tf_op | source)
XLA Modules:
  0.0 133.3 jit_solution(7510956113457762981)
XLA Ops:
  0.0 4.8 %states.1 = (bf16[32,48,128]{2,1,0:T(8,128)(2,1)}, f32[8,1024]{1,0:T(8,128)}, f32[1024,128]{1,0:T(8,128)}, s32[1,1024]{1,0:T(1,128)}) custom-call(s32[1,1024]{1,0:T(1,128)} %bitcast.17, s32[1,1024]{1,0:T(1,128)} %bitcast.18, bf16[1024,512]{1,0:T(8,128)(2,1)} %q.3, bf16[1024,512]{1,0:T(8,128)(2,1)} %k.7, bf16[1024,512]{1,0:T(8,128)(2,1)} %v.7, ...), custom_call_target="tpu_custom_call" | custom-call | tf_op jit(solution)/shard_map/states/pallas_call | solution.py:222
  4.8 11.9 %all-to-all-start = ((bf16[32,48,128]{2,1,0:T(8,128)(2,1)}), bf16[32,48,128]{2,1,0:T(8,128)(2,1)S(1)}, u32[]{:S(2)}, u32[]{:S(2)}) async-start(bf16[32,48,128]{2,1,0:T(8,128)(2,1)} %get-tuple-element.15), calls=%async_computation | async-start | bytes 786432 | tf_op jit(solution)/shard_map/all_to_all | solution.py:242
  16.8 0.0 copy-start.1
  16.8 0.7 copy-done.1
  17.5 13.9 %local.1 = (f32[4,3,1024,128]{3,2,1,0:T(8,128)}, f32[8,128]{1,0:T(8,128)S(1)}) custom-call(f32[8,1024]{1,0:T(8,128)S(1)} %copy-done.1, f32[1024,128]{1,0:T(8,128)} %get-tuple-element.14.seg_col, bf16[1024,512]{1,0:T(8,128)(2,1)} %q.3, bf16[1024,512]{1,0:T(8,128)(2,1)} %k.7, bf16[1024,512]{1,0:T(8,128)(2,1)} %v.7, bf16[1024,512]{1,0:T(8,128)(2,1)} %g.7), custom_call_target="tpu_custom_call" | custom-call | flops 4294967296 | bytes 10485760 | tf_op jit(solution)/shard_map/local/pallas_call | solution.py:244
  31.4 0.0 all-to-all-done.got
  31.4 0.8 chain.1
  32.2 9.2 %all-to-all-start.1 = ((bf16[32,32,128]{2,1,0:T(8,128)(2,1)}), bf16[32,32,128]{2,1,0:T(8,128)(2,1)S(1)}, u32[]{:S(2)}, u32[]{:S(2)}) async-start(bf16[32,32,128]{2,1,0:T(8,128)(2,1)} %chain.1), calls=%async_computation.1 | async-start | bytes 524288 | tf_op jit(solution)/shard_map/all_to_all | solution.py:270
  41.5 0.1 pad_add_fusion.1.targets
  41.5 10.7 %ahead.1 = (f32[2,3,256,512]{3,2,1,0:T(8,128)}, bf16[2,3,256,512]{3,2,1,0:T(8,128)(2,1)}) custom-call(s32[2]{0:T(128)S(1)} %pad_add_fusion.1.targets, f32[1024,128]{1,0:T(8,128)} %get-tuple-element.14.seg_col, s32[1,1024]{1,0:T(1,128)} %get-tuple-element.13.dest, f32[4,3,1024,128]{3,2,1,0:T(8,128)} %get-tuple-element.18.local, bf16[1024,512]{1,0:T(8,128)(2,1)} %k.7, ...), custom_call_target="tpu_custom_call" | custom-call | flops 4831838208 | bytes 1048576 | tf_op jit(solution)/shard_map/ahead/pallas_call | solution.py:291
  52.2 0.0 all-to-all-done.1.states
  52.2 2.9 %finish.3 = bf16[3,256,512]{2,1,0:T(8,128)(2,1)} custom-call(f32[2,3,256,512]{3,2,1,0:T(8,128)} %get-tuple-element.19.kept_q.kept_k.kept_v, f32[2,3,256,512]{3,2,1,0:T(8,128)} %get-tuple-element.19.kept_q.kept_k.kept_v, f32[2,3,256,512]{3,2,1,0:T(8,128)} %get-tuple-element.19.kept_q.kept_k.kept_v, ...), custom_call_target="tpu_custom_call" | custom-call | flops 100663296 | bytes 1048576 | tf_op jit(solution)/shard_map/finish/pallas_call | solution.py:322
  55.1 5.3 %collective-permute-start.6 = (bf16[3,256,512]{2,1,0:T(8,128)(2,1)}, bf16[3,256,512]{2,1,0:T(8,128)(2,1)}, u32[]{:S(2)}, u32[]{:S(2)}) collective-permute-start(bf16[3,256,512]{2,1,0:T(8,128)(2,1)} %finish.3), channel_id=1, source_target_pairs={{0,5},{1,4},{2,7},{3,6},{4,1},{5,0},{6,3},{7,2},{8,13},{9,12},{10,... | collective-permute-start | bytes 2359304 | tf_op jit(solution)/shard_map/ppermute | solution.py:384
  60.4 2.9 %finish.2 = bf16[3,256,512]{2,1,0:T(8,128)(2,1)} custom-call(f32[2,3,256,512]{3,2,1,0:T(8,128)} %get-tuple-element.19.kept_q.kept_k.kept_v, f32[2,3,256,512]{3,2,1,0:T(8,128)} %get-tuple-element.19.kept_q.kept_k.kept_v, f32[2,3,256,512]{3,2,1,0:T(8,128)} %get-tuple-element.19.kept_q.kept_k.kept_v, ...), custom_call_target="tpu_custom_call" | custom-call | flops 100663296 | bytes 1048576 | tf_op jit(solution)/shard_map/finish/pallas_call | solution.py:322
  63.4 0.1 collective-permute-start.5
  63.4 0.0 copy-start
  63.4 5.1 %combine.1.grads = bf16[3,1024,512]{2,1,0:T(8,128)(2,1)S(1)} custom-call(f32[1024,128]{1,0:T(8,128)} %get-tuple-element.14.seg_col, bf16[32,32,128]{2,1,0:T(8,128)(2,1)S(1)} %all-to-all-done.1.states, f32[4,3,1024,128]{3,2,1,0:T(8,128)} %get-tuple-element.18.local, bf16[1024,512]{1,0:T(8,128)(2,1)} %k.7, bf16[1024,512]{1,0:T(8,128)(2,1)} %v.7, ...), custom_call_target="tpu_custom_call" | custom-call | flops 402653184 | bytes 1048576 | tf_op jit(solution)/shard_map/combine/pallas_call | solution.py:336
  68.5 0.0 copy-done
  68.5 1.9 %place.9 = bf16[3,256,512]{2,1,0:T(8,128)(2,1)} custom-call(s32[1]{0:T(128)} %bitcast.10.target, s32[1,1024]{1,0:T(1,128)S(1)} %copy-done, bf16[3,1024,512]{2,1,0:T(8,128)(2,1)S(1)} %combine.1.grads), custom_call_target="tpu_custom_call" | custom-call | flops 805306368 | bytes 1048576 | tf_op jit(solution)/shard_map/place/pallas_call | solution.py:373
  70.4 1.0 collective-permute-start.3
  71.4 1.9 %place.7 = bf16[3,256,512]{2,1,0:T(8,128)(2,1)} custom-call(s32[1]{0:T(128)} %bitcast.8.target, s32[1,1024]{1,0:T(1,128)S(1)} %copy-done, bf16[3,1024,512]{2,1,0:T(8,128)(2,1)S(1)} %combine.1.grads), custom_call_target="tpu_custom_call" | custom-call | flops 805306368 | bytes 1048576 | tf_op jit(solution)/shard_map/place/pallas_call | solution.py:373
  73.3 1.7 %collective-permute-start.1 = (bf16[3,256,512]{2,1,0:T(8,128)(2,1)}, bf16[3,256,512]{2,1,0:T(8,128)(2,1)}, u32[]{:S(2)}, u32[]{:S(2)}) collective-permute-start(bf16[3,256,512]{2,1,0:T(8,128)(2,1)} %place.7), channel_id=1, source_target_pairs={{0,6},{1,7},{2,0},{3,1},{4,2},{5,3},{6,4},{7,5},{8,14},{9,15},{10,... | collective-permute-start | bytes 2359304 | tf_op jit(solution)/shard_map/ppermute | solution.py:384
  75.0 1.9 %place.8 = bf16[3,256,512]{2,1,0:T(8,128)(2,1)} custom-call(s32[1]{0:T(128)} %bitcast.9.target, s32[1,1024]{1,0:T(1,128)S(1)} %copy-done, bf16[3,1024,512]{2,1,0:T(8,128)(2,1)S(1)} %combine.1.grads), custom_call_target="tpu_custom_call" | custom-call | flops 805306368 | bytes 1048576 | tf_op jit(solution)/shard_map/place/pallas_call | solution.py:373
  76.9 2.0 %collective-permute-start.2 = (bf16[3,256,512]{2,1,0:T(8,128)(2,1)}, bf16[3,256,512]{2,1,0:T(8,128)(2,1)}, u32[]{:S(2)}, u32[]{:S(2)}) collective-permute-start(bf16[3,256,512]{2,1,0:T(8,128)(2,1)} %place.8), channel_id=1, source_target_pairs={{0,3},{1,2},{2,5},{3,4},{4,7},{5,6},{6,1},{7,0},{8,11},{9,10},{10,... | collective-permute-start | bytes 2359304 | tf_op jit(solution)/shard_map/ppermute | solution.py:384
  78.9 1.9 %place.10 = bf16[3,256,512]{2,1,0:T(8,128)(2,1)} custom-call(s32[1]{0:T(128)} %bitcast.4.target, s32[1,1024]{1,0:T(1,128)S(1)} %copy-done, bf16[3,1024,512]{2,1,0:T(8,128)(2,1)S(1)} %combine.1.grads), custom_call_target="tpu_custom_call" | custom-call | flops 805306368 | bytes 1048576 | tf_op jit(solution)/shard_map/place/pallas_call | solution.py:373
  80.9 1.9 %place.6 = bf16[3,256,512]{2,1,0:T(8,128)(2,1)} custom-call(s32[1]{0:T(128)} %bitcast.5.target, s32[1,1024]{1,0:T(1,128)S(1)} %copy-done, bf16[3,1024,512]{2,1,0:T(8,128)(2,1)S(1)} %combine.1.grads), custom_call_target="tpu_custom_call" | custom-call | flops 805306368 | bytes 1048576 | tf_op jit(solution)/shard_map/place/pallas_call | solution.py:373
  82.7 0.0 collective-permute-done.6.refs_1_
  82.7 0.0 collective-permute-start.4
  82.7 12.8 %collective-permute-done.5.refs_0_ = bf16[3,256,512]{2,1,0:T(8,128)(2,1)} collective-permute-done((bf16[3,256,512]{2,1,0:T(8,128)(2,1)}, bf16[3,256,512]{2,1,0:T(8,128)(2,1)}, u32[]{:S(2)}, u32[]{:S(2)}) %collective-permute-start.5) | collective-permute-done | bytes 786464 | tf_op jit(solution)/shard_map/ppermute | solution.py:384
  95.6 1.2 collective-permute-start
  96.7 0.1 stack.57.sources
  96.8 0.1 pad_add_fusion.sources
  96.9 1.9 %place.11.refs_2_ = bf16[3,256,4096]{2,1,0:T(8,128)(2,1)} custom-call(s32[1]{0:T(128)} %bitcast.15.target, s32[1,1024]{1,0:T(1,128)S(1)} %copy-done, bf16[3,1024,512]{2,1,0:T(8,128)(2,1)S(1)} %combine.1.grads), custom_call_target="tpu_custom_call" | custom-call | flops 805306368 | bytes 1048576 | tf_op jit(solution)/shard_map/place/pallas_call | solution.py:360
  98.8 2.8 %unpack.2.refs_5_ = bf16[3,256,4096]{2,1,0:T(8,128)(2,1)} custom-call(s32[2]{0:T(128)S(1)} %pad_add_fusion.sources, bf16[3,256,512]{2,1,0:T(8,128)(2,1)} %collective-permute-done.5.refs_0_, bf16[3,256,512]{2,1,0:T(8,128)(2,1)} %collective-permute-done.6.refs_1_, bf16[3,256,4096]{2,1,0:T(8,128)(2,1)} %place.11.refs_2_), custom_call_target="tpu_custom_call", output_to_operand_aliasing={{}: (3, {})} | custom-call | bytes 1048576 | tf_op jit(solution)/shard_map/unpack/pallas_call | solution.py:394
  101.6 8.5 %collective-permute-done.3.refs_3_ = bf16[3,256,512]{2,1,0:T(8,128)(2,1)} collective-permute-done((bf16[3,256,512]{2,1,0:T(8,128)(2,1)}, bf16[3,256,512]{2,1,0:T(8,128)(2,1)}, u32[]{:S(2)}, u32[]{:S(2)}) %collective-permute-start.3) | collective-permute-done | bytes 786464 | tf_op jit(solution)/shard_map/ppermute | solution.py:384
  110.1 18.0 %collective-permute-done.1.refs_1_ = bf16[3,256,512]{2,1,0:T(8,128)(2,1)} collective-permute-done((bf16[3,256,512]{2,1,0:T(8,128)(2,1)}, bf16[3,256,512]{2,1,0:T(8,128)(2,1)}, u32[]{:S(2)}, u32[]{:S(2)}) %collective-permute-start.1) | collective-permute-done | bytes 786464 | tf_op jit(solution)/shard_map/ppermute | solution.py:384
  128.1 0.0 collective-permute-done.2.refs_2_
  128.1 0.0 collective-permute-done.4.refs_4_
  128.1 1.3 collective-permute-done.refs_0_
  129.4 3.7 %unpack.3 = bf16[3,256,4096]{2,1,0:T(8,128)(2,1)} custom-call(s32[5]{0:T(128)S(1)} %stack.57.sources, bf16[3,256,512]{2,1,0:T(8,128)(2,1)} %collective-permute-done.refs_0_, bf16[3,256,512]{2,1,0:T(8,128)(2,1)} %collective-permute-done.1.refs_1_, bf16[3,256,512]{2,1,0:T(8,128)(2,1)} %collective-permute-done.2.refs_2_, ...), custom_call_target="tpu_custom_call", output_to_operand_aliasing={{}: (6, {})} | custom-call | bytes 1048576 | tf_op jit(solution)/shard_map/unpack/pallas_call | solution.py:394
Async XLA Ops:
  4.8 26.6 %all-to-all-start = ((bf16[32,48,128]{2,1,0:T(8,128)(2,1)}), bf16[32,48,128]{2,1,0:T(8,128)(2,1)S(1)}, u32[]{:S(2)}, u32[]{:S(2)}) async-start(bf16[32,48,128]{2,1,0:T(8,128)(2,1)} %get-tuple-element.15), calls=%async_computation | async-start | bytes 786432 | tf_op jit(solution)/shard_map/all_to_all | solution.py:242
  16.8 0.8 copy-start.1
  32.2 20.0 %all-to-all-start.1 = ((bf16[32,32,128]{2,1,0:T(8,128)(2,1)}), bf16[32,32,128]{2,1,0:T(8,128)(2,1)S(1)}, u32[]{:S(2)}, u32[]{:S(2)}) async-start(bf16[32,32,128]{2,1,0:T(8,128)(2,1)} %chain.1), calls=%async_computation.1 | async-start | bytes 524288 | tf_op jit(solution)/shard_map/all_to_all | solution.py:270
  55.1 27.6 %collective-permute-start.6 = (bf16[3,256,512]{2,1,0:T(8,128)(2,1)}, bf16[3,256,512]{2,1,0:T(8,128)(2,1)}, u32[]{:S(2)}, u32[]{:S(2)}) collective-permute-start(bf16[3,256,512]{2,1,0:T(8,128)(2,1)} %finish.3), channel_id=1, source_target_pairs={{0,5},{1,4},{2,7},{3,6},{4,1},{5,0},{6,3},{7,2},{8,13},{9,12},{10,... | collective-permute-start | bytes 2359304 | tf_op jit(solution)/shard_map/ppermute | solution.py:384
  63.4 32.2 %collective-permute-start.5 = (bf16[3,256,512]{2,1,0:T(8,128)(2,1)}, bf16[3,256,512]{2,1,0:T(8,128)(2,1)}, u32[]{:S(2)}, u32[]{:S(2)}) collective-permute-start(bf16[3,256,512]{2,1,0:T(8,128)(2,1)} %finish.2), channel_id=1, source_target_pairs={{0,4},{1,5},{2,6},{3,7},{4,0},{5,1},{6,2},{7,3},{8,12},{9,13},{10,... | collective-permute-start | bytes 2359304 | tf_op jit(solution)/shard_map/ppermute | solution.py:384
  63.4 5.1 %copy-start = (s32[1,1024]{1,0:T(1,128)S(1)}, s32[1,1024]{1,0:T(1,128)}, u32[]{:S(2)}) copy-start(s32[1,1024]{1,0:T(1,128)} %get-tuple-element.13.dest) | copy-start | bytes 12292
  70.4 39.7 %collective-permute-start.3 = (bf16[3,256,512]{2,1,0:T(8,128)(2,1)}, bf16[3,256,512]{2,1,0:T(8,128)(2,1)}, u32[]{:S(2)}, u32[]{:S(2)}) collective-permute-start(bf16[3,256,512]{2,1,0:T(8,128)(2,1)} %place.9), channel_id=1, source_target_pairs={{0,7},{1,6},{2,1},{3,0},{4,3},{5,2},{6,5},{7,4},{8,15},{9,14},{10,... | collective-permute-start | bytes 2359304 | tf_op jit(solution)/shard_map/ppermute | solution.py:384
  73.3 54.8 %collective-permute-start.1 = (bf16[3,256,512]{2,1,0:T(8,128)(2,1)}, bf16[3,256,512]{2,1,0:T(8,128)(2,1)}, u32[]{:S(2)}, u32[]{:S(2)}) collective-permute-start(bf16[3,256,512]{2,1,0:T(8,128)(2,1)} %place.7), channel_id=1, source_target_pairs={{0,6},{1,7},{2,0},{3,1},{4,2},{5,3},{6,4},{7,5},{8,14},{9,15},{10,... | collective-permute-start | bytes 2359304 | tf_op jit(solution)/shard_map/ppermute | solution.py:384
  76.9 51.2 %collective-permute-start.2 = (bf16[3,256,512]{2,1,0:T(8,128)(2,1)}, bf16[3,256,512]{2,1,0:T(8,128)(2,1)}, u32[]{:S(2)}, u32[]{:S(2)}) collective-permute-start(bf16[3,256,512]{2,1,0:T(8,128)(2,1)} %place.8), channel_id=1, source_target_pairs={{0,3},{1,2},{2,5},{3,4},{4,7},{5,6},{6,1},{7,0},{8,11},{9,10},{10,... | collective-permute-start | bytes 2359304 | tf_op jit(solution)/shard_map/ppermute | solution.py:384
  82.7 45.4 %collective-permute-start.4 = (bf16[3,256,512]{2,1,0:T(8,128)(2,1)}, bf16[3,256,512]{2,1,0:T(8,128)(2,1)}, u32[]{:S(2)}, u32[]{:S(2)}) collective-permute-start(bf16[3,256,512]{2,1,0:T(8,128)(2,1)} %place.10), channel_id=1, source_target_pairs={{0,1},{1,0},{2,3},{3,2},{4,5},{5,4},{6,7},{7,6},{8,9},{9,8},{10,11... | collective-permute-start | bytes 2359304 | tf_op jit(solution)/shard_map/ppermute | solution.py:384
  95.6 33.9 %collective-permute-start = (bf16[3,256,512]{2,1,0:T(8,128)(2,1)}, bf16[3,256,512]{2,1,0:T(8,128)(2,1)}, u32[]{:S(2)}, u32[]{:S(2)}) collective-permute-start(bf16[3,256,512]{2,1,0:T(8,128)(2,1)} %place.6), channel_id=1, source_target_pairs={{0,2},{1,3},{2,4},{3,5},{4,6},{5,7},{6,0},{7,1},{8,10},{9,11},{10,... | collective-permute-start | bytes 2359304 | tf_op jit(solution)/shard_map/ppermute | solution.py:384

commit v3 on v2

v3 whole, which is shorter than its diff:
```python
import functools

import jax
import jax.numpy as jnp
from jax import lax
from jax.experimental import pallas as pl
from jax.experimental.pallas import tpu as pltpu
from jax.sharding import PartitionSpec as P

HD = 128
TILE = 256
F32 = jnp.float32
BF16 = jnp.bfloat16


def dot_nn(a, b):
    return lax.dot_general(a, b, (((1,), (0,)), ((), ())), preferred_element_type=F32)


def dot_nt(a, b):
    return lax.dot_general(a, b, (((1,), (1,)), ((), ())), preferred_element_type=F32)


def dot_tn(a, b):
    return lax.dot_general(a, b, (((0,), (0,)), ((), ())), preferred_element_type=F32)


def params(steps=1, mebibytes=24):
    return pltpu.CompilerParams(
        dimension_semantics=("arbitrary",) * steps, vmem_limit_bytes=mebibytes << 20
    )


def states_body(count, capacity, starts, owners, q, k, v, g, pay, seg_row, seg_col, dest):
    span = starts.shape[1]

    @pl.when(pl.program_id(0) == 0)
    def _():
        begin = starts[...]
        owner = owners[...]
        rows = lax.broadcasted_iota(jnp.int32, (count + 8, span), 0)
        hit = jnp.where(rows < count, owner, begin) == jnp.where(rows < count, rows, 1)
        hit = hit.astype(F32)
        lanes = range(0, span, HD)
        stack = jnp.concatenate([hit[:, at : at + HD] for at in lanes], axis=0).astype(BF16)
        before = (
            lax.broadcasted_iota(jnp.int32, (HD, HD), 0)
            <= lax.broadcasted_iota(jnp.int32, (HD, HD), 1)
        ).astype(F32).astype(BF16)
        inner = dot_nn(stack, before)
        whole = dot_nn(stack, jnp.ones((HD, HD), BF16))
        offset = jnp.zeros((count + 8, HD), F32)
        for turn, at in enumerate(lanes):
            mine = slice(turn * (count + 8), (turn + 1) * (count + 8))
            sums = inner[mine] + offset
            offset = offset + whole[mine]
            seg_row[:, at : at + HD] = sums[count:]
            slot = jnp.sum(
                hit[:count, at : at + HD] * (sums[:count] - 1.0), axis=0, keepdims=True
            )
            dest[:, at : at + HD] = owner[:, at : at + HD] * capacity + slot.astype(jnp.int32)
            seg_col[at : at + HD, :] = jnp.broadcast_to(sums[count : count + 1], (HD, HD)).T

    segment = seg_col[...]
    total = segment[span - 1 :, :]
    first = (segment == 0.0).astype(F32).astype(BF16)
    last = (segment == total).astype(F32).astype(BF16)
    pieces = pay.shape[0]
    part = HD // pieces
    fwd = dot_tn(k[...] * last, v[...]).astype(BF16)
    bwd = dot_tn(q[...] * first, g[...]).astype(BF16)
    pay[:, :part, :] = fwd.reshape(pieces, part, HD)
    pay[:, part : 2 * part, :] = bwd.reshape(pieces, part, HD)
    keep = (total == 0.0).astype(F32)
    pay[:, 2 * part :, :] = jnp.broadcast_to(keep[None], (pieces, 16, HD)).astype(BF16)


def chain_body(count, part, got, after, out, token):
    token[...] = after[...]
    fwd = jnp.zeros((part, HD), F32)
    bwd = jnp.zeros((part, HD), F32)
    for turn in range(count):
        out[turn, :part, :] = fwd.astype(BF16)
        keep = got[turn, 2 * part : 2 * part + 1, :].astype(F32)
        fwd = got[turn, :part, :].astype(F32) + keep * fwd
        back = count - 1 - turn
        out[back, part:, :] = bwd.astype(BF16)
        keep = got[back, 2 * part : 2 * part + 1, :].astype(F32)
        bwd = got[back, part : 2 * part, :].astype(F32) + keep * bwd


def local_body(ahead, target, after, seg_row, seg_col, dest, q, k, v, g, *refs):
    if ahead:
        out, token, kept, raw, mask, mask_t, sums, sems, pick = refs
    else:
        out, token, mask, mask_t, sums, sems = refs
    span = q.shape[0]
    turn_now = pl.program_id(0)

    @pl.when(turn_now == 0)
    def _():
        token[...] = after[...]
        shape = (TILE, TILE)
        here = lax.broadcasted_iota(jnp.int32, shape, 0)
        there = lax.broadcasted_iota(jnp.int32, shape, 1)
        for lo in range(0, span, TILE):
            hi = lo + TILE
            col = seg_col[lo:hi, :1]
            same = col == seg_row[:1, lo:hi]
            mask[lo:hi, lo:hi] = (same & (there <= here)).astype(F32).astype(BF16)
            mask_t[lo:hi, lo:hi] = (same & (there >= here)).astype(F32).astype(BF16)
            if lo:
                mask[lo:hi, :lo] = (col == seg_row[:1, :lo]).astype(F32).astype(BF16)
            if hi < span:
                mask_t[lo:hi, hi:] = (col == seg_row[:1, hi:]).astype(F32).astype(BF16)
        if ahead:
            pick[...] = pick_rows(dest, target[0], pick.shape[0])

    def add(kind, rows, term, fresh):
        if fresh:
            sums[turn_now, kind] = term
        else:
            sums[turn_now, kind, rows, :] += term

    def write(turn, kind):
        return pltpu.make_async_copy(
            sums.at[turn, kind], out.at[turn, kind], sems.at[turn, kind]
        )

    for lo in range(0, span, TILE):
        hi = lo + TILE
        score = dot_nt(g[lo:, :], v[lo:hi, :]).astype(BF16) * mask[lo:, lo:hi]
        add(0, slice(lo, span), dot_nn(score, k[lo:hi, :]), lo == 0)
    write(turn_now, 0).start()
    for kind, left, right, other in ((1, v, g, q), (2, k, q, g)):
        for hi in range(span, 0, -TILE):
            lo = hi - TILE
            score = dot_nt(left[:hi, :], right[lo:hi, :]).astype(BF16) * mask_t[:hi, lo:hi]
            add(kind, slice(0, hi), dot_nn(score, other[lo:hi, :]), hi == span)
        write(turn_now, kind).start()

    if ahead:
        first, last = edges(seg_col)
        first, last = first.astype(BF16), last.astype(BF16)
        exact = [sums[turn_now, kind] for kind in range(3)]
        high = [part.astype(BF16) for part in exact]
        low = [(part - near.astype(F32)).astype(BF16) for part, near in zip(exact, high)]
        rows = [g[...] * first, v[...] * last, k[...] * last]
        moved = dot_nn(pick[...], jnp.concatenate(high + low + rows, axis=1))
        for kind in range(3):
            at = kind * HD
            kept[kind] = moved[:, at : at + HD] + moved[:, 3 * HD + at : 4 * HD + at]
            raw[kind] = moved[:, 6 * HD + at : 7 * HD + at].astype(BF16)

    @pl.when(turn_now == pl.num_programs(0) - 1)
    def _():
        for turn in range(sums.shape[0]):
            for kind in range(3):
                write(turn, kind).wait()


def pick_rows(dest, owner, capacity):
    shape = (capacity, dest.shape[1])
    slots = owner * capacity + lax.broadcasted_iota(jnp.int32, shape, 0)
    return (dest[...] == slots).astype(F32).astype(BF16)


def edges(seg_col):
    segment = seg_col[...]
    first = (segment == 0.0).astype(F32)
    last = (segment == segment[segment.shape[0] - 1 :, :]).astype(F32)
    return first, last


def term_of(states, head, part, kind, rows):
    pieces = HD // part
    mine = slice(head * pieces, (head + 1) * pieces)
    if kind == 0:
        return dot_nt(rows, states[mine, :part, :].reshape(HD, HD))
    bwd = states[mine, part:, :].reshape(HD, HD)
    return dot_nt(rows, bwd) if kind == 1 else dot_nn(rows, bwd)


def finish_body(part, kept_q, kept_k, kept_v, raw_q, raw_k, raw_v, states, after, out, token):
    token[...] = after[...]
    for head in range(out.shape[2] // HD):
        own = slice(head * HD, (head + 1) * HD)
        pairs = ((kept_q, raw_q), (kept_k, raw_k), (kept_v, raw_v))
        for kind, (kept, raw) in enumerate(pairs):
            term = term_of(states, head, part, kind, raw[0, :, own])
            out[kind, :, own] = (kept[0, :, own] + term).astype(BF16)


def combine_body(
    part, half, target, after, seg_col, dest, states, early, late, k, v, g, grads, out, pick
):
    del after
    head = pl.program_id(0)

    @pl.when(head == 0)
    def _():
        pick[...] = pick_rows(dest, target[0], pick.shape[0])

    first, last = edges(seg_col)
    own = pl.ds(pl.multiple_of(head * HD, HD), HD)
    for kind, (edge, rows) in enumerate(((first, g), (last, v), (last, k))):
        term = term_of(states, 0, part, kind, rows[...])
        base = jnp.where(head < half, early[0, kind], late[0, kind])
        grads[kind, :, own] = (base + edge * term).astype(BF16)

    @pl.when(head >= half)
    def _():
        for kind in range(3):
            out[kind] = dot_nn(pick[...], grads[kind, :, own]).astype(BF16)


def place_body(lo, target, dest, grads, *refs):
    out = refs[-1]
    pick = pick_rows(dest, target[0], out.shape[1])
    for kind in range(3):
        out[kind] = dot_nn(pick, grads[kind, :, lo:]).astype(BF16)


def unpack_body(feats, starts, sources, *refs):
    many = len(starts)
    out, sems, out_sems = refs[many + 1 : many + 4]
    held = refs[many + 4 :]
    loads, stores = [], []
    for turn in range(many):
        loads.append(pltpu.make_async_copy(refs[turn], held[turn], sems.at[turn]))
        loads[-1].start()
    for turn, lo in enumerate(starts):
        loads[turn].wait()
        width = held[turn].shape[2]
        cols = pl.ds(pl.multiple_of(sources[turn] * feats + lo, HD), width)
        stores.append(
            pltpu.make_async_copy(held[turn], out.at[:, :, cols], out_sems.at[turn])
        )
        stores[-1].start()
    for store in stores:
        store.wait()


def shards(queries, keys, values, out_grad, starts, owners):
    span, feats = queries.shape
    heads = feats // HD
    n_seq = lax.axis_size("seq")
    count = lax.axis_size("head")
    capacity = 2 * span // count
    part = heads * HD // n_seq
    pieces = HD // part
    full = lambda *shape: pl.BlockSpec(shape, lambda i: (0,) * len(shape))
    by_head = pl.BlockSpec((span, HD), lambda i: (0, i))
    whole = pl.BlockSpec(memory_space=pltpu.VMEM)
    smem = pl.BlockSpec(memory_space=pltpu.SMEM)
    hbm = lambda array: pltpu.with_memory_space_constraint(array, pltpu.HBM)
    in_hbm = [hbm(array) for array in (queries, keys, values, out_grad)]
    starts_row = starts.reshape(1, span)
    owners_row = owners.reshape(1, span)

    payload, seg_row, seg_col, dest = pl.pallas_call(
        functools.partial(states_body, count, capacity),
        grid=(heads,),
        in_specs=[full(1, span), full(1, span)] + [by_head] * 4,
        out_specs=[
            pl.BlockSpec((pieces, 2 * part + 16, HD), lambda i: (i, 0, 0)),
            full(8, span),
            full(span, HD),
            full(1, span),
        ],
        out_shape=[
            jax.ShapeDtypeStruct((n_seq, 2 * part + 16, HD), BF16),
            jax.ShapeDtypeStruct((8, span), F32),
            jax.ShapeDtypeStruct((span, HD), F32),
            jax.ShapeDtypeStruct((1, span), jnp.int32),
        ],
        compiler_params=params(1, 60),
        name="states",
    )(starts_row, owners_row, *in_hbm)

    gathered = lax.all_to_all(payload, "seq", 0, 0, tiled=True)

    me = lax.axis_index("head")
    rows = count // 2
    hops = [(rows // 2, 0), (rows // 2, 1)]
    far = len(hops)
    for step in range(1, rows // 2):
        hops += [(step, 0), (rows - step, 0)]
    hops += [(0, 1)]
    for step in range(1, rows // 2):
        hops += [(step, 1), (rows - step, 1)]
    hops += [(0, 0)]

    def moved(index, hop, sign):
        row = (index // 2 + sign * hop[0]) % rows
        return row * 2 + (index % 2 + hop[1]) % 2

    def scalars(*indices):
        return jnp.stack([index.astype(jnp.int32) for index in indices])

    fixed = lambda *shape: pl.BlockSpec(shape, lambda i, *t: (0,) * len(shape))
    raw_block = pl.BlockSpec((span, HD), lambda i, *t: (0, i))

    def local_half(half, after):
        base = half * (heads // 2)
        ahead = half == 0
        by = pl.BlockSpec((span, HD), lambda i, t: (0, base + i))
        block = pl.BlockSpec((3, capacity, HD), lambda i, t: (0, 0, i))
        return pl.pallas_call(
            functools.partial(local_body, ahead),
            grid_spec=pltpu.PrefetchScalarGridSpec(
                num_scalar_prefetch=1,
                grid=(heads // 2,),
                in_specs=[fixed(8, HD), fixed(8, span), fixed(span, HD), fixed(1, span)] + [by] * 4,
                out_specs=[pl.BlockSpec(memory_space=pl.ANY), fixed(8, HD)] + [block] * 2 * ahead,
                scratch_shapes=[pltpu.VMEM((span, span), BF16)] * 2
                + [
                    pltpu.VMEM((heads // 2, 3, span, HD), F32),
                    pltpu.SemaphoreType.DMA((heads // 2, 3)),
                ]
                + [pltpu.VMEM((capacity, span), BF16)] * ahead,
            ),
            out_shape=[
                pltpu.HBM((heads // 2, 3, span, HD), F32),
                jax.ShapeDtypeStruct((8, HD), F32),
            ]
            + [
                pltpu.HBM((3, capacity, feats // 2), F32),
                pltpu.HBM((3, capacity, feats // 2), BF16),
            ]
            * ahead,
            compiler_params=params(),
            cost_estimate=pl.CostEstimate(
                flops=heads * 6 * span * span * HD, bytes_accessed=10 << 20, transcendentals=0
            ),
            name="local",
        )(
            scalars(moved(me, hops[0], 1)),
            after,
            hbm(seg_row),
            hbm(seg_col),
            hbm(dest),
            *in_hbm,
        )

    early, token, kept, raw = local_half(0, hbm(seg_row))

    chained, token = pl.pallas_call(
        functools.partial(chain_body, n_seq, part),
        in_specs=[whole] * 2,
        out_specs=[whole, whole],
        out_shape=[
            jax.ShapeDtypeStruct((n_seq, 2 * part, HD), BF16),
            jax.ShapeDtypeStruct((8, HD), F32),
        ],
        compiler_params=params(0),
        name="chain",
    )(gathered, token)

    states = lax.all_to_all(chained, "seq", 0, 0, tiled=True)

    late, token = local_half(1, token)
    light = pl.CostEstimate(flops=1, bytes_accessed=1, transcendentals=0)

    blocks = [
        pl.BlockSpec((1, capacity, feats // 2), lambda i, kind=kind: (kind, 0, 0))
        for kind in range(3)
    ]
    chunk, token = pl.pallas_call(
        functools.partial(finish_body, part),
        grid=(1,),
        in_specs=blocks * 2 + [whole, whole],
        out_specs=[whole, whole],
        out_shape=[
            pltpu.VMEM((3, capacity, feats // 2), BF16),
            pltpu.VMEM((8, HD), F32),
        ],
        compiler_params=params(),
        cost_estimate=light,
        name="finish",
    )(*[hbm(kept)] * 3, *[hbm(raw)] * 3, states, token)

    def combine(after):
        half = heads // 2
        by_half = [
            pl.BlockSpec((1, 3, span, HD), lambda i, t: (jnp.minimum(i, half - 1), 0, 0, 0)),
            pl.BlockSpec((1, 3, span, HD), lambda i, t: (jnp.maximum(i - half, 0), 0, 0, 0)),
        ]
        return pl.pallas_call(
            functools.partial(combine_body, part, half),
            grid_spec=pltpu.PrefetchScalarGridSpec(
                num_scalar_prefetch=1,
                grid=(heads,),
                in_specs=[
                    whole,
                    fixed(span, HD),
                    fixed(1, span),
                    pl.BlockSpec((pieces, 2 * part, HD), lambda i, t: (i, 0, 0)),
                ]
                + by_half
                + [raw_block] * 3,
                out_specs=[
                    whole,
                    pl.BlockSpec((3, capacity, HD), lambda i, t: (0, 0, jnp.maximum(i - half, 0))),
                ],
                scratch_shapes=[pltpu.VMEM((capacity, span), BF16)],
            ),
            out_shape=[
                pltpu.VMEM((3, span, feats), BF16),
                jax.ShapeDtypeStruct((3, capacity, feats // 2), BF16),
            ],
            compiler_params=params(1),
            cost_estimate=light,
            name="combine",
        )(
            scalars(moved(me, hops[0], 1)),
            after,
            hbm(seg_col),
            hbm(dest),
            states,
            hbm(early),
            hbm(late),
            *in_hbm[1:],
        )

    def place(hop, grads, lo=0, after=()):
        later = [pl.BlockSpec(memory_space=pl.ANY)] * len(after)
        target = scalars(moved(me, hop, 1))
        if hop == (0, 0):
            return pl.pallas_call(
                functools.partial(place_body, lo),
                grid_spec=pltpu.PrefetchScalarGridSpec(
                    num_scalar_prefetch=1,
                    grid=(1,),
                    in_specs=[whole] * 2 + later,
                    out_specs=pl.BlockSpec((3, capacity, feats), lambda i, t: (0, 0, t[0])),
                ),
                out_shape=jax.ShapeDtypeStruct((3, capacity, count * feats), BF16),
                compiler_params=params(),
                cost_estimate=light,
                name="place",
            )(target, dest, grads, *after)
        return pl.pallas_call(
            functools.partial(place_body, lo),
            in_specs=[smem] + [whole] * 2 + later,
            out_specs=whole,
            out_shape=pltpu.VMEM((3, capacity, feats - lo), BF16),
            compiler_params=params(0),
            cost_estimate=light,
            name="place",
        )(target, dest, grads, *after)

    def sent(chunk, hop):
        return lax.ppermute(
            chunk, "head", [(index, moved(index, hop, 1)) for index in range(count)]
        )

    middle = feats // 2
    parts = [(hops[0], 0), (hops[0], middle)]
    received = [sent(chunk, hops[0])]
    grads, chunk = combine(token)
    received.append(sent(chunk, hops[0]))
    for hop in hops[1:-1]:
        parts.append((hop, 0))
        behind = received[0 if hops.index(hop) < far + 9 else 1]
        received.append(sent(place(hop, grads, 0, (hbm(behind),)), hop))
    result = place(hops[-1], grads, 0, (hbm(received[0]),))
    groups = ((0, far + 1), (far + 1, len(parts) - 2), (len(parts) - 2, len(parts)))
    for lo, hi in groups:
        many = hi - lo
        result = pl.pallas_call(
            functools.partial(unpack_body, feats, [start for _, start in parts[lo:hi]]),
            in_specs=[smem] + [pl.BlockSpec(memory_space=pl.ANY)] * (many + 1),
            out_specs=pl.BlockSpec(memory_space=pl.ANY),
            out_shape=jax.ShapeDtypeStruct((3, capacity, count * feats), BF16),
            scratch_shapes=[
                pltpu.SemaphoreType.DMA((many,)),
                pltpu.SemaphoreType.DMA((many,)),
            ]
            + [pltpu.VMEM(one.shape, BF16) for one in received[lo:hi]],
            input_output_aliases={many + 1: 0},
            compiler_params=params(0, 16),
            cost_estimate=light,
            name="unpack",
        )(
            scalars(*[moved(me, hop, -1) for hop, _ in parts[lo:hi]]),
            *[hbm(one) for one in received[lo:hi]],
            result,
        )
    return jnp.transpose(result, (1, 0, 2))


def solution(mesh):
    in_specs = (
        P("seq", "head"),
        P("seq", "head"),
        P("seq", "head"),
        P("seq", "head"),
        P("seq"),
        P("seq", None),
    )
    out_specs = P(("seq", "head"), None, None)
    return jax.shard_map(
        shards,
        mesh=mesh,
        in_specs=in_specs,
        out_specs=out_specs,
        check_vma=False,
    )
```

time: 134 us -> 132 us (0.985)
  Pallas kernels: 58.9 us -> 54.8 us
  starting transfers between devices: 32.4 us -> 35.8 us
    ppermute x7 -> x8, starting transfers between devices: 11.3 us -> 15.8 us  [sent(): lax.ppermute(chunk, 'head', [(index, moved(index, hop, 1)) for index in r...]
    pallas_call x13 -> x14, Pallas kernels: 53.3 us -> 49.2 us  [the longest x2 17.9 us: local_half(): pl.pallas_call(functools.partial(local_body, ahead), grid_spec=pltpu.Pref...]
    ppermute x7 -> x8, waiting for transfers between devices: 40.6 us -> 36.6 us  [sent(): lax.ppermute(chunk, 'head', [(index, moved(index, hop, 1)) for index in r...]
    all_to_all x1, waiting for transfers between devices: 0.01 us -> 2.19 us  [shards(): states = lax.all_to_all(chained, 'seq', 0, 0, tiled=True)]
  transfers between devices with their start and end apart: 9 -> 10, of which waited for: 4 -> 6; matrix products, arithmetic and copies ran while one was open for 0% -> 0% of each run, Pallas kernels for 35% -> 32%
where the time goes in v3:
time: 132 us; the launch traced here: 131 us
  Pallas kernels  54.8 us (42%)
  waiting for transfers between devices  39.9 us (30%)
  starting transfers between devices  35.8 us (27%)
    ppermute x8, waiting for transfers between devices, sent(): lax.ppermute(chunk, 'head', [(index, moved(index, hop, 1)) for index in r...  36.6 us
    pallas_call x2, Pallas kernels, local_half(): pl.pallas_call(functools.partial(local_body, ahead), grid_spec=pltpu.Pref...  17.9 us
    ppermute x8, starting transfers between devices, sent(): lax.ppermute(chunk, 'head', [(index, moved(index, hop, 1)) for index in r...  15.8 us
    all_to_all x1, starting transfers between devices, shards(): gathered = lax.all_to_all(payload, 'seq', 0, 0, tiled=True)  11.9 us
    pallas_call x6, Pallas kernels, place(): pl.pallas_call(functools.partial(place_body, lo), in_specs=[smem] + [whol...  11.3 us
    pallas_call x3, Pallas kernels, shards(): pl.pallas_call(functools.partial(unpack_body, feats, [start for _, start...  8.81 us
    all_to_all x1, starting transfers between devices, shards(): states = lax.all_to_all(chained, 'seq', 0, 0, tiled=True)  8.11 us
    pallas_call x1, Pallas kernels, combine(): pl.pallas_call(functools.partial(combine_body, part, half), grid_spec=plt...  6.97 us
  transfers between devices with their start and end apart: 10, of which 6 were waited for; matrix products, arithmetic and copies ran while one was open for 0% of the time, Pallas kernels for 32%

profile of v3, /device:TPU:1, one launch (start us, length us, event | category | flops | bytes accessed | tf_op | source)
XLA Modules:
  0.0 131.0 jit_solution(5788253218857614306)
XLA Ops:
  0.0 4.8 %states.1 = (bf16[32,48,128]{2,1,0:T(8,128)(2,1)}, f32[8,1024]{1,0:T(8,128)}, f32[1024,128]{1,0:T(8,128)}, s32[1,1024]{1,0:T(1,128)}) custom-call(s32[1,1024]{1,0:T(1,128)} %bitcast.17, s32[1,1024]{1,0:T(1,128)} %bitcast.18, bf16[1024,512]{1,0:T(8,128)(2,1)} %q.5, bf16[1024,512]{1,0:T(8,128)(2,1)} %k.7, bf16[1024,512]{1,0:T(8,128)(2,1)} %v.7, ...), custom_call_target="tpu_custom_call" | custom-call | tf_op jit(solution)/shard_map/states/pallas_call | solution.py:261
  4.8 11.9 %all-to-all-start = ((bf16[32,48,128]{2,1,0:T(8,128)(2,1)}), bf16[32,48,128]{2,1,0:T(8,128)(2,1)S(1)}, u32[]{:S(2)}, u32[]{:S(2)}) async-start(bf16[32,48,128]{2,1,0:T(8,128)(2,1)} %get-tuple-element.26), calls=%async_computation | async-start | bytes 786432 | tf_op jit(solution)/shard_map/all_to_all | solution.py:281
  16.8 10.5 %local.2 = (f32[2,3,1024,128]{3,2,1,0:T(8,128)}, f32[8,128]{1,0:T(8,128)S(1)}, f32[3,256,256]{2,1,0:T(8,128)}, bf16[3,256,256]{2,1,0:T(8,128)(2,1)}) custom-call(s32[1]{0:T(128)} %bitcast.5.target, f32[8,1024]{1,0:T(8,128)} %get-tuple-element.22.after.seg_row, f32[8,1024]{1,0:T(8,128)} %get-tuple-element.22.after.seg_row, ...), custom_call_target="tpu_custom_call" | custom-call | flops 3221225472 | bytes 10485760 | tf_op jit(solution)/shard_map/local/pallas_call | solution.py:309
  27.2 1.1 all-to-all-done.got
  28.4 0.8 chain.1
  29.1 8.1 %all-to-all-start.1 = ((bf16[32,32,128]{2,1,0:T(8,128)(2,1)}), bf16[32,32,128]{2,1,0:T(8,128)(2,1)S(1)}, u32[]{:S(2)}, u32[]{:S(2)}) async-start(bf16[32,32,128]{2,1,0:T(8,128)(2,1)} %get-tuple-element.28), calls=%async_computation.1 | async-start | bytes 524288 | tf_op jit(solution)/shard_map/all_to_all | solution.py:360
  37.3 7.5 %local.3 = (f32[2,3,1024,128]{3,2,1,0:T(8,128)}, f32[8,128]{1,0:T(8,128)S(1)}) custom-call(s32[1]{0:T(128)} %bitcast.5.target, f32[8,128]{1,0:T(8,128)S(1)} %get-tuple-element.29.after, f32[8,1024]{1,0:T(8,128)} %get-tuple-element.22.after.seg_row, f32[1024,128]{1,0:T(8,128)} %get-tuple-element.23.seg_col, s32[1,1024]{1,0:T(1,128)} %get-tuple-element.21.dest, ...), custom_call_target="tpu_custom_call" | custom-call | flops 3221225472 | bytes 10485760 | tf_op jit(solution)/shard_map/local/pallas_call | solution.py:309
  44.7 2.2 %all-to-all-done.1.states = bf16[32,32,128]{2,1,0:T(8,128)(2,1)S(1)} async-done(((bf16[32,32,128]{2,1,0:T(8,128)(2,1)}), bf16[32,32,128]{2,1,0:T(8,128)(2,1)S(1)}, u32[]{:S(2)}, u32[]{:S(2)}) %all-to-all-start.1) | async-done | bytes 262176 | tf_op jit(solution)/shard_map/all_to_all | solution.py:360
  46.9 0.0 copy-start
  46.9 2.3 %finish.1 = (bf16[3,256,256]{2,1,0:T(8,128)(2,1)}, f32[8,128]{1,0:T(8,128)S(1)}) custom-call(f32[3,256,256]{2,1,0:T(8,128)} %get-tuple-element.24.kept_q.kept_k.kept_v, f32[3,256,256]{2,1,0:T(8,128)} %get-tuple-element.24.kept_q.kept_k.kept_v, f32[3,256,256]{2,1,0:T(8,128)} %get-tuple-element.24.kept_q.kept_k.kept_v, ...), custom_call_target="tpu_custom_call" | custom-call | flops 1 | bytes 1 | tf_op jit(solution)/shard_map/finish/pallas_call | solution.py:369
  49.2 2.9 %collective-permute-start = (bf16[3,256,256]{2,1,0:T(8,128)(2,1)}, bf16[3,256,256]{2,1,0:T(8,128)(2,1)}, u32[]{:S(2)}, u32[]{:S(2)}) collective-permute-start(bf16[3,256,256]{2,1,0:T(8,128)(2,1)} %get-tuple-element.35), channel_id=1, source_target_pairs={{0,4},{1,5},{2,6},{3,7},{4,0},{5,1},{6,2},{7,3},{8,12},{9,13},{10,... | collective-permute-start | bytes 1179656 | tf_op jit(solution)/shard_map/ppermute | solution.py:454
  52.1 7.0 %combine.1 = (bf16[3,1024,512]{2,1,0:T(8,128)(2,1)S(1)}, bf16[3,256,256]{2,1,0:T(8,128)(2,1)}) custom-call(s32[1]{0:T(128)} %bitcast.5.target, f32[8,128]{1,0:T(8,128)S(1)} %get-tuple-element.31.after, f32[1024,128]{1,0:T(8,128)} %get-tuple-element.23.seg_col, s32[1,1024]{1,0:T(1,128)} %get-tuple-element.21.dest, ...), custom_call_target="tpu_custom_call" | custom-call | flops 1 | bytes 1 | tf_op jit(solution)/shard_map/combine/pallas_call | solution.py:389
  59.1 0.0 collective-permute-done.refs_0_
  59.1 0.0 copy-done
  59.1 1.9 %place.12 = bf16[3,256,512]{2,1,0:T(8,128)(2,1)} custom-call(s32[1]{0:T(128)} %bitcast.14.target, s32[1,1024]{1,0:T(1,128)S(1)} %copy-done, bf16[3,1024,512]{2,1,0:T(8,128)(2,1)S(1)} %get-tuple-element.34.grads, bf16[3,256,256]{2,1,0:T(8,128)(2,1)} %collective-permute-done.refs_0_), custom_call_target="tpu_custom_call" | custom-call | flops 1 | bytes 1 | tf_op jit(solution)/shard_map/place/pallas_call | solution.py:443
  61.0 6.3 %collective-permute-start.7 = (bf16[3,256,512]{2,1,0:T(8,128)(2,1)}, bf16[3,256,512]{2,1,0:T(8,128)(2,1)}, u32[]{:S(2)}, u32[]{:S(2)}) collective-permute-start(bf16[3,256,512]{2,1,0:T(8,128)(2,1)} %place.12), channel_id=1, source_target_pairs={{0,5},{1,4},{2,7},{3,6},{4,1},{5,0},{6,3},{7,2},{8,13},{9,12},{10,... | collective-permute-start | bytes 2359304 | tf_op jit(solution)/shard_map/ppermute | solution.py:454
  67.2 0.5 collective-permute-start.6
  67.7 1.9 %place.9 = bf16[3,256,512]{2,1,0:T(8,128)(2,1)} custom-call(s32[1]{0:T(128)} %bitcast.10.target, s32[1,1024]{1,0:T(1,128)S(1)} %copy-done, bf16[3,1024,512]{2,1,0:T(8,128)(2,1)S(1)} %get-tuple-element.34.grads, bf16[3,256,256]{2,1,0:T(8,128)(2,1)} %collective-permute-done.refs_0_), custom_call_target="tpu_custom_call" | custom-call | flops 1 | bytes 1 | tf_op jit(solution)/shard_map/place/pallas_call | solution.py:443
  69.6 0.9 collective-permute-start.3
  70.5 1.9 %place.10 = bf16[3,256,512]{2,1,0:T(8,128)(2,1)} custom-call(s32[1]{0:T(128)} %bitcast.11.target, s32[1,1024]{1,0:T(1,128)S(1)} %copy-done, bf16[3,1024,512]{2,1,0:T(8,128)(2,1)S(1)} %get-tuple-element.34.grads, bf16[3,256,256]{2,1,0:T(8,128)(2,1)} %collective-permute-done.refs_0_), custom_call_target="tpu_custom_call" | custom-call | flops 1 | bytes 1 | tf_op jit(solution)/shard_map/place/pallas_call | solution.py:443
  72.3 1.8 %collective-permute-start.4 = (bf16[3,256,512]{2,1,0:T(8,128)(2,1)}, bf16[3,256,512]{2,1,0:T(8,128)(2,1)}, u32[]{:S(2)}, u32[]{:S(2)}) collective-permute-start(bf16[3,256,512]{2,1,0:T(8,128)(2,1)} %place.10), channel_id=1, source_target_pairs={{0,6},{1,7},{2,0},{3,1},{4,2},{5,3},{6,4},{7,5},{8,14},{9,15},{10,... | collective-permute-start | bytes 2359304 | tf_op jit(solution)/shard_map/ppermute | solution.py:454
  74.1 1.9 %place.11 = bf16[3,256,512]{2,1,0:T(8,128)(2,1)} custom-call(s32[1]{0:T(128)} %bitcast.9.target, s32[1,1024]{1,0:T(1,128)S(1)} %copy-done, bf16[3,1024,512]{2,1,0:T(8,128)(2,1)S(1)} %get-tuple-element.34.grads, bf16[3,256,256]{2,1,0:T(8,128)(2,1)} %collective-permute-done.refs_0_), custom_call_target="tpu_custom_call" | custom-call | flops 1 | bytes 1 | tf_op jit(solution)/shard_map/place/pallas_call | solution.py:443
  76.0 0.5 collective-permute-start.5
  76.6 1.9 %place.8 = bf16[3,256,512]{2,1,0:T(8,128)(2,1)} custom-call(s32[1]{0:T(128)} %bitcast.6.target, s32[1,1024]{1,0:T(1,128)S(1)} %copy-done, bf16[3,1024,512]{2,1,0:T(8,128)(2,1)S(1)} %get-tuple-element.34.grads, bf16[3,256,256]{2,1,0:T(8,128)(2,1)} %collective-permute-done.refs_0_), custom_call_target="tpu_custom_call" | custom-call | flops 1 | bytes 1 | tf_op jit(solution)/shard_map/place/pallas_call | solution.py:443
  78.4 1.9 %place.7 = bf16[3,256,512]{2,1,0:T(8,128)(2,1)} custom-call(s32[1]{0:T(128)} %bitcast.2.target, s32[1,1024]{1,0:T(1,128)S(1)} %copy-done, bf16[3,1024,512]{2,1,0:T(8,128)(2,1)S(1)} %get-tuple-element.34.grads, bf16[3,256,256]{2,1,0:T(8,128)(2,1)} %collective-permute-done.refs_0_), custom_call_target="tpu_custom_call" | custom-call | flops 1 | bytes 1 | tf_op jit(solution)/shard_map/place/pallas_call | solution.py:443
  80.3 13.9 %collective-permute-done.6.refs_1_ = bf16[3,256,256]{2,1,0:T(8,128)(2,1)} collective-permute-done((bf16[3,256,256]{2,1,0:T(8,128)(2,1)}, bf16[3,256,256]{2,1,0:T(8,128)(2,1)}, u32[]{:S(2)}, u32[]{:S(2)}) %collective-permute-start.6) | collective-permute-done | bytes 393248 | tf_op jit(solution)/shard_map/ppermute | solution.py:454
  94.3 0.2 collective-permute-start.1
  94.5 0.0 collective-permute-done.7.refs_2_
  94.5 2.7 %collective-permute-start.2 = (bf16[3,256,512]{2,1,0:T(8,128)(2,1)}, bf16[3,256,512]{2,1,0:T(8,128)(2,1)}, u32[]{:S(2)}, u32[]{:S(2)}) collective-permute-start(bf16[3,256,512]{2,1,0:T(8,128)(2,1)} %place.8), channel_id=1, source_target_pairs={{0,7},{1,6},{2,1},{3,0},{4,3},{5,2},{6,5},{7,4},{8,15},{9,14},{10,... | collective-permute-start | bytes 2359304 | tf_op jit(solution)/shard_map/ppermute | solution.py:454
  97.2 0.1 pad_add_fusion.sources
  97.3 0.1 pad_add_fusion.2.sources
  97.4 1.9 %place.13.refs_3_ = bf16[3,256,4096]{2,1,0:T(8,128)(2,1)} custom-call(s32[1]{0:T(128)} %bitcast.15.target, s32[1,1024]{1,0:T(1,128)S(1)} %copy-done, bf16[3,1024,512]{2,1,0:T(8,128)(2,1)S(1)} %get-tuple-element.34.grads, bf16[3,256,256]{2,1,0:T(8,128)(2,1)} %collective-permute-done.refs_0_), custom_call_target="tpu_custom_call" | custom-call | flops 1 | bytes 1 | tf_op jit(solution)/shard_map/place/pallas_call | solution.py:430
  99.3 0.1 pad_add_fusion.1.sources
  99.3 2.8 %unpack.3.refs_3_ = bf16[3,256,4096]{2,1,0:T(8,128)(2,1)} custom-call(s32[3]{0:T(128)S(1)} %pad_add_fusion.2.sources, bf16[3,256,256]{2,1,0:T(8,128)(2,1)} %collective-permute-done.refs_0_, bf16[3,256,256]{2,1,0:T(8,128)(2,1)} %collective-permute-done.6.refs_1_, bf16[3,256,512]{2,1,0:T(8,128)(2,1)} %collective-permute-done.7.refs_2_, ...), custom_call_target="tpu_custom_call", output_to_operand_aliasing={{}: (4, {})} | custom-call | flops 1 | bytes 1 | tf_op jit(solution)/shard_map/unpack/pallas_call | solution.py:471
  102.2 9.0 %collective-permute-done.3.refs_0_ = bf16[3,256,512]{2,1,0:T(8,128)(2,1)} collective-permute-done((bf16[3,256,512]{2,1,0:T(8,128)(2,1)}, bf16[3,256,512]{2,1,0:T(8,128)(2,1)}, u32[]{:S(2)}, u32[]{:S(2)}) %collective-permute-start.3) | collective-permute-done | bytes 786464 | tf_op jit(solution)/shard_map/ppermute | solution.py:454
  111.2 0.2 collective-permute-done.4.refs_1_
  111.4 0.0 collective-permute-done.5.refs_2_
  111.4 3.1 %unpack.4.refs_2_ = bf16[3,256,4096]{2,1,0:T(8,128)(2,1)} custom-call(s32[3]{0:T(128)S(1)} %pad_add_fusion.1.sources, bf16[3,256,512]{2,1,0:T(8,128)(2,1)} %collective-permute-done.3.refs_0_, bf16[3,256,512]{2,1,0:T(8,128)(2,1)} %collective-permute-done.4.refs_1_, ...), custom_call_target="tpu_custom_call", output_to_operand_aliasing={{}: (4, {})} | custom-call | flops 1 | bytes 1 | tf_op jit(solution)/shard_map/unpack/pallas_call | solution.py:471
  114.5 13.5 %collective-permute-done.1.refs_0_ = bf16[3,256,512]{2,1,0:T(8,128)(2,1)} collective-permute-done((bf16[3,256,512]{2,1,0:T(8,128)(2,1)}, bf16[3,256,512]{2,1,0:T(8,128)(2,1)}, u32[]{:S(2)}, u32[]{:S(2)}) %collective-permute-start.1) | collective-permute-done | bytes 786464 | tf_op jit(solution)/shard_map/ppermute | solution.py:454
  128.0 0.0 collective-permute-done.2.refs_1_
  128.0 2.8 %unpack.5 = bf16[3,256,4096]{2,1,0:T(8,128)(2,1)} custom-call(s32[2]{0:T(128)S(1)} %pad_add_fusion.sources, bf16[3,256,512]{2,1,0:T(8,128)(2,1)} %collective-permute-done.1.refs_0_, bf16[3,256,512]{2,1,0:T(8,128)(2,1)} %collective-permute-done.2.refs_1_, bf16[3,256,4096]{2,1,0:T(8,128)(2,1)} %unpack.4.refs_2_), custom_call_target="tpu_custom_call", output_to_operand_aliasing={{}: (3, {})} | custom-call | flops 1 | bytes 1 | tf_op jit(solution)/shard_map/unpack/pallas_call | solution.py:471
Async XLA Ops:
  4.8 23.5 %all-to-all-start = ((bf16[32,48,128]{2,1,0:T(8,128)(2,1)}), bf16[32,48,128]{2,1,0:T(8,128)(2,1)S(1)}, u32[]{:S(2)}, u32[]{:S(2)}) async-start(bf16[32,48,128]{2,1,0:T(8,128)(2,1)} %get-tuple-element.26), calls=%async_computation | async-start | bytes 786432 | tf_op jit(solution)/shard_map/all_to_all | solution.py:281
  29.1 17.8 %all-to-all-start.1 = ((bf16[32,32,128]{2,1,0:T(8,128)(2,1)}), bf16[32,32,128]{2,1,0:T(8,128)(2,1)S(1)}, u32[]{:S(2)}, u32[]{:S(2)}) async-start(bf16[32,32,128]{2,1,0:T(8,128)(2,1)} %get-tuple-element.28), calls=%async_computation.1 | async-start | bytes 524288 | tf_op jit(solution)/shard_map/all_to_all | solution.py:360
  46.9 12.2 %copy-start = (s32[1,1024]{1,0:T(1,128)S(1)}, s32[1,1024]{1,0:T(1,128)}, u32[]{:S(2)}) copy-start(s32[1,1024]{1,0:T(1,128)} %get-tuple-element.21.dest) | copy-start | bytes 12292
  49.2 9.9 %collective-permute-start = (bf16[3,256,256]{2,1,0:T(8,128)(2,1)}, bf16[3,256,256]{2,1,0:T(8,128)(2,1)}, u32[]{:S(2)}, u32[]{:S(2)}) collective-permute-start(bf16[3,256,256]{2,1,0:T(8,128)(2,1)} %get-tuple-element.35), channel_id=1, source_target_pairs={{0,4},{1,5},{2,6},{3,7},{4,0},{5,1},{6,2},{7,3},{8,12},{9,13},{10,... | collective-permute-start | bytes 1179656 | tf_op jit(solution)/shard_map/ppermute | solution.py:454
  61.0 33.6 %collective-permute-start.7 = (bf16[3,256,512]{2,1,0:T(8,128)(2,1)}, bf16[3,256,512]{2,1,0:T(8,128)(2,1)}, u32[]{:S(2)}, u32[]{:S(2)}) collective-permute-start(bf16[3,256,512]{2,1,0:T(8,128)(2,1)} %place.12), channel_id=1, source_target_pairs={{0,5},{1,4},{2,7},{3,6},{4,1},{5,0},{6,3},{7,2},{8,13},{9,12},{10,... | collective-permute-start | bytes 2359304 | tf_op jit(solution)/shard_map/ppermute | solution.py:454
  67.2 27.1 %collective-permute-start.6 = (bf16[3,256,256]{2,1,0:T(8,128)(2,1)}, bf16[3,256,256]{2,1,0:T(8,128)(2,1)}, u32[]{:S(2)}, u32[]{:S(2)}) collective-permute-start(bf16[3,256,256]{2,1,0:T(8,128)(2,1)} %get-tuple-element.36), channel_id=1, source_target_pairs={{0,4},{1,5},{2,6},{3,7},{4,0},{5,1},{6,2},{7,3},{8,12},{9,13},{10,... | collective-permute-start | bytes 1179656 | tf_op jit(solution)/shard_map/ppermute | solution.py:454
  69.6 41.6 %collective-permute-start.3 = (bf16[3,256,512]{2,1,0:T(8,128)(2,1)}, bf16[3,256,512]{2,1,0:T(8,128)(2,1)}, u32[]{:S(2)}, u32[]{:S(2)}) collective-permute-start(bf16[3,256,512]{2,1,0:T(8,128)(2,1)} %place.9), channel_id=1, source_target_pairs={{0,2},{1,3},{2,4},{3,5},{4,6},{5,7},{6,0},{7,1},{8,10},{9,11},{10,... | collective-permute-start | bytes 2359304 | tf_op jit(solution)/shard_map/ppermute | solution.py:454
  72.3 39.1 %collective-permute-start.4 = (bf16[3,256,512]{2,1,0:T(8,128)(2,1)}, bf16[3,256,512]{2,1,0:T(8,128)(2,1)}, u32[]{:S(2)}, u32[]{:S(2)}) collective-permute-start(bf16[3,256,512]{2,1,0:T(8,128)(2,1)} %place.10), channel_id=1, source_target_pairs={{0,6},{1,7},{2,0},{3,1},{4,2},{5,3},{6,4},{7,5},{8,14},{9,15},{10,... | collective-permute-start | bytes 2359304 | tf_op jit(solution)/shard_map/ppermute | solution.py:454
  76.0 35.4 %collective-permute-start.5 = (bf16[3,256,512]{2,1,0:T(8,128)(2,1)}, bf16[3,256,512]{2,1,0:T(8,128)(2,1)}, u32[]{:S(2)}, u32[]{:S(2)}) collective-permute-start(bf16[3,256,512]{2,1,0:T(8,128)(2,1)} %place.11), channel_id=1, source_target_pairs={{0,1},{1,0},{2,3},{3,2},{4,5},{5,4},{6,7},{7,6},{8,9},{9,8},{10,11... | collective-permute-start | bytes 2359304 | tf_op jit(solution)/shard_map/ppermute | solution.py:454
  94.3 33.7 %collective-permute-start.1 = (bf16[3,256,512]{2,1,0:T(8,128)(2,1)}, bf16[3,256,512]{2,1,0:T(8,128)(2,1)}, u32[]{:S(2)}, u32[]{:S(2)}) collective-permute-start(bf16[3,256,512]{2,1,0:T(8,128)(2,1)} %place.7), channel_id=1, source_target_pairs={{0,3},{1,2},{2,5},{3,4},{4,7},{5,6},{6,1},{7,0},{8,11},{9,10},{10,... | collective-permute-start | bytes 2359304 | tf_op jit(solution)/shard_map/ppermute | solution.py:454
  94.5 33.5 %collective-permute-start.2 = (bf16[3,256,512]{2,1,0:T(8,128)(2,1)}, bf16[3,256,512]{2,1,0:T(8,128)(2,1)}, u32[]{:S(2)}, u32[]{:S(2)}) collective-permute-start(bf16[3,256,512]{2,1,0:T(8,128)(2,1)} %place.8), channel_id=1, source_target_pairs={{0,7},{1,6},{2,1},{3,0},{4,3},{5,2},{6,5},{7,4},{8,15},{9,14},{10,... | collective-permute-start | bytes 2359304 | tf_op jit(solution)/shard_map/ppermute | solution.py:454

commit v4 on v3

--- a/solution.py
+++ b/solution.py
@@ -92,8 +92,10 @@
 def local_body(ahead, target, after, seg_row, seg_col, dest, q, k, v, g, *refs):
     if ahead:
         out, token, kept, raw, mask, mask_t, sums, sems, pick = refs
+        base = 0
     else:
-        out, token, mask, mask_t, sums, sems = refs
+        out, token, mask, mask_t, sums, sems = refs[1:]
+        base = sums.shape[0]
     span = q.shape[0]
     turn_now = pl.program_id(0)
 
@@ -124,7 +126,7 @@
 
     def write(turn, kind):
         return pltpu.make_async_copy(
-            sums.at[turn, kind], out.at[turn, kind], sems.at[turn, kind]
+            sums.at[turn, kind], out.at[base + turn, kind], sems.at[turn, kind]
         )
 
     for lo in range(0, span, TILE):
@@ -192,26 +194,32 @@
 
 
 def combine_body(
-    part, half, target, after, seg_col, dest, states, early, late, k, v, g, grads, out, pick
+    part, half, targets, after, seg_col, dest, states, local, k, v, g, grads, rest, other, pick
 ):
     del after
     head = pl.program_id(0)
 
     @pl.when(head == 0)
     def _():
-        pick[...] = pick_rows(dest, target[0], pick.shape[0])
+        for turn in range(2):
+            pick[turn] = pick_rows(dest, targets[turn], pick.shape[1])
 
     first, last = edges(seg_col)
     own = pl.ds(pl.multiple_of(head * HD, HD), HD)
     for kind, (edge, rows) in enumerate(((first, g), (last, v), (last, k))):
         term = term_of(states, 0, part, kind, rows[...])
-        base = jnp.where(head < half, early[0, kind], late[0, kind])
-        grads[kind, :, own] = (base + edge * term).astype(BF16)
+        grads[kind, :, own] = (local[0, kind] + edge * term).astype(BF16)
+
+    now = jnp.concatenate([grads[kind, :, own] for kind in range(3)], axis=1)
+    moved = dot_nn(pick[1], now).astype(BF16)
+    for kind in range(3):
+        other[kind] = moved[:, kind * HD : (kind + 1) * HD]
 
     @pl.when(head >= half)
     def _():
+        moved = dot_nn(pick[0], now).astype(BF16)
         for kind in range(3):
-            out[kind] = dot_nn(pick[...], grads[kind, :, own]).astype(BF16)
+            rest[kind] = moved[:, kind * HD : (kind + 1) * HD]
 
 
 def place_body(lo, target, dest, grads, *refs):
@@ -301,7 +309,7 @@
     fixed = lambda *shape: pl.BlockSpec(shape, lambda i, *t: (0,) * len(shape))
     raw_block = pl.BlockSpec((span, HD), lambda i, *t: (0, i))
 
-    def local_half(half, after):
+    def local_half(half, after, *earlier):
         base = half * (heads // 2)
         ahead = half == 0
         by = pl.BlockSpec((span, HD), lambda i, t: (0, base + i))
@@ -311,7 +319,9 @@
             grid_spec=pltpu.PrefetchScalarGridSpec(
                 num_scalar_prefetch=1,
                 grid=(heads // 2,),
-                in_specs=[fixed(8, HD), fixed(8, span), fixed(span, HD), fixed(1, span)] + [by] * 4,
+                in_specs=[fixed(8, HD), fixed(8, span), fixed(span, HD), fixed(1, span)]
+                + [by] * 4
+                + [pl.BlockSpec(memory_space=pl.ANY)] * len(earlier),
                 out_specs=[pl.BlockSpec(memory_space=pl.ANY), fixed(8, HD)] + [block] * 2 * ahead,
                 scratch_shapes=[pltpu.VMEM((span, span), BF16)] * 2
                 + [
@@ -321,7 +331,7 @@
                 + [pltpu.VMEM((capacity, span), BF16)] * ahead,
             ),
             out_shape=[
-                pltpu.HBM((heads // 2, 3, span, HD), F32),
+                pltpu.HBM((heads, 3, span, HD), F32),
                 jax.ShapeDtypeStruct((8, HD), F32),
             ]
             + [
@@ -329,6 +339,7 @@
                 pltpu.HBM((3, capacity, feats // 2), BF16),
             ]
             * ahead,
+            input_output_aliases={9: 0} if earlier else {},
             compiler_params=params(),
             cost_estimate=pl.CostEstimate(
                 flops=heads * 6 * span * span * HD, bytes_accessed=10 << 20, transcendentals=0
@@ -341,6 +352,7 @@
             hbm(seg_col),
             hbm(dest),
             *in_hbm,
+            *earlier,
         )
 
     early, token, kept, raw = local_half(0, hbm(seg_row))
@@ -359,7 +371,7 @@
 
     states = lax.all_to_all(chained, "seq", 0, 0, tiled=True)
 
-    late, token = local_half(1, token)
+    local, token = local_half(1, token, hbm(early))
     light = pl.CostEstimate(flops=1, bytes_accessed=1, transcendentals=0)
 
     blocks = [
@@ -382,10 +394,6 @@
 
     def combine(after):
         half = heads // 2
-        by_half = [
-            pl.BlockSpec((1, 3, span, HD), lambda i, t: (jnp.minimum(i, half - 1), 0, 0, 0)),
-            pl.BlockSpec((1, 3, span, HD), lambda i, t: (jnp.maximum(i - half, 0), 0, 0, 0)),
-        ]
         return pl.pallas_call(
             functools.partial(combine_body, part, half),
             grid_spec=pltpu.PrefetchScalarGridSpec(
@@ -396,30 +404,31 @@
                     fixed(span, HD),
                     fixed(1, span),
                     pl.BlockSpec((pieces, 2 * part, HD), lambda i, t: (i, 0, 0)),
+                    pl.BlockSpec((1, 3, span, HD), lambda i, t: (i, 0, 0, 0)),
                 ]
-                + by_half
                 + [raw_block] * 3,
                 out_specs=[
                     whole,
                     pl.BlockSpec((3, capacity, HD), lambda i, t: (0, 0, jnp.maximum(i - half, 0))),
+                    pl.BlockSpec((3, capacity, HD), lambda i, t: (0, 0, i)),
                 ],
-                scratch_shapes=[pltpu.VMEM((capacity, span), BF16)],
+                scratch_shapes=[pltpu.VMEM((2, capacity, span), BF16)],
             ),
             out_shape=[
                 pltpu.VMEM((3, span, feats), BF16),
                 jax.ShapeDtypeStruct((3, capacity, feats // 2), BF16),
+                jax.ShapeDtypeStruct((3, capacity, feats), BF16),
             ],
             compiler_params=params(1),
             cost_estimate=light,
             name="combine",
         )(
-            scalars(moved(me, hops[0], 1)),
+            scalars(*[moved(me, hop, 1) for hop in hops[:2]]),
             after,
             hbm(seg_col),
             hbm(dest),
             states,
-            hbm(early),
-            hbm(late),
+            hbm(local),
             *in_hbm[1:],
         )
 
@@ -456,14 +465,14 @@
         )
 
     middle = feats // 2
-    parts = [(hops[0], 0), (hops[0], middle)]
+    parts = [(hops[0], 0), (hops[0], middle), (hops[1], 0)]
     received = [sent(chunk, hops[0])]
-    grads, chunk = combine(token)
-    received.append(sent(chunk, hops[0]))
-    for hop in hops[1:-1]:
+    grads, rest, other = combine(token)
+    other, _ = lax.optimization_barrier((other, received[0]))
+    received += [sent(rest, hops[0]), sent(other, hops[1])]
+    for hop in hops[2:-1]:
         parts.append((hop, 0))
-        behind = received[0 if hops.index(hop) < far + 9 else 1]
-        received.append(sent(place(hop, grads, 0, (hbm(behind),)), hop))
+        received.append(sent(place(hop, grads, 0, (hbm(received[0]),)), hop))
     result = place(hops[-1], grads, 0, (hbm(received[0]),))
     groups = ((0, far + 1), (far + 1, len(parts) - 2), (len(parts) - 2, len(parts)))
     for lo, hi in groups:

time: 132 us -> 130 us (0.985)
  waiting for transfers between devices: 39.9 us -> 38.4 us
    pallas_call x6 -> x5, Pallas kernels: 11.3 us -> 9.43 us  [place(): pl.pallas_call(functools.partial(place_body, lo), in_specs=[smem] + [whol...]
    pallas_call x1, Pallas kernels: 6.97 us -> 8.81 us  [combine(): pl.pallas_call(functools.partial(combine_body, part, half), grid_spec=plt...]
    ppermute x8, waiting for transfers between devices: 36.6 us -> 35.1 us  [sent(): lax.ppermute(chunk, 'head', [(index, moved(index, hop, 1)) for index in r...]
  transfers between devices with their start and end apart: 10 -> 10, of which waited for: 6 -> 6; matrix products, arithmetic and copies ran while one was open for 0% -> 0% of each run, Pallas kernels for 32% -> 34%
where the time goes in v4:
time: 130 us; the launch traced here: 129 us
  Pallas kernels  54.8 us (42%)
  waiting for transfers between devices  38.4 us (30%)
  starting transfers between devices  35.4 us (27%)
    ppermute x8, waiting for transfers between devices, sent(): lax.ppermute(chunk, 'head', [(index, moved(index, hop, 1)) for index in r...  35.1 us
    pallas_call x2, Pallas kernels, local_half(): pl.pallas_call(functools.partial(local_body, ahead), grid_spec=pltpu.Pref...  18 us
    ppermute x8, starting transfers between devices, sent(): lax.ppermute(chunk, 'head', [(index, moved(index, hop, 1)) for index in r...  15.4 us
    all_to_all x1, starting transfers between devices, shards(): gathered = lax.all_to_all(payload, 'seq', 0, 0, tiled=True)  11.9 us
    pallas_call x5, Pallas kernels, place(): pl.pallas_call(functools.partial(place_body, lo), in_specs=[smem] + [whol...  9.43 us
    pallas_call x3, Pallas kernels, shards(): pl.pallas_call(functools.partial(unpack_body, feats, [start for _, start...  8.81 us
    pallas_call x1, Pallas kernels, combine(): pl.pallas_call(functools.partial(combine_body, part, half), grid_spec=plt...  8.81 us
    all_to_all x1, starting transfers between devices, shards(): states = lax.all_to_all(chained, 'seq', 0, 0, tiled=True)  8.16 us
  transfers between devices with their start and end apart: 10, of which 6 were waited for; matrix products, arithmetic and copies ran while one was open for 0% of the time, Pallas kernels for 34%

profile of v4, /device:TPU:1, one launch (start us, length us, event | category | flops | bytes accessed | tf_op | source)
XLA Modules:
  0.0 129.1 jit_solution(16141667181011022512)
XLA Ops:
  0.0 4.8 %states.1 = (bf16[32,48,128]{2,1,0:T(8,128)(2,1)}, f32[8,1024]{1,0:T(8,128)}, f32[1024,128]{1,0:T(8,128)}, s32[1,1024]{1,0:T(1,128)}) custom-call(s32[1,1024]{1,0:T(1,128)} %bitcast.17, s32[1,1024]{1,0:T(1,128)} %bitcast.18, bf16[1024,512]{1,0:T(8,128)(2,1)} %q.5, bf16[1024,512]{1,0:T(8,128)(2,1)} %k.7, bf16[1024,512]{1,0:T(8,128)(2,1)} %v.7, ...), custom_call_target="tpu_custom_call" | custom-call | tf_op jit(solution)/shard_map/states/pallas_call | solution.py:269
  4.8 11.9 %all-to-all-start = ((bf16[32,48,128]{2,1,0:T(8,128)(2,1)}), bf16[32,48,128]{2,1,0:T(8,128)(2,1)S(1)}, u32[]{:S(2)}, u32[]{:S(2)}) async-start(bf16[32,48,128]{2,1,0:T(8,128)(2,1)} %get-tuple-element.28), calls=%async_computation | async-start | bytes 786432 | tf_op jit(solution)/shard_map/all_to_all | solution.py:289
  16.8 10.5 %local.2 = (f32[4,3,1024,128]{3,2,1,0:T(8,128)}, f32[8,128]{1,0:T(8,128)S(1)}, f32[3,256,256]{2,1,0:T(8,128)}, bf16[3,256,256]{2,1,0:T(8,128)(2,1)}) custom-call(s32[1]{0:T(128)} %bitcast.5.target, f32[8,1024]{1,0:T(8,128)} %get-tuple-element.24.after.seg_row, f32[8,1024]{1,0:T(8,128)} %get-tuple-element.24.after.seg_row, ...), custom_call_target="tpu_custom_call" | custom-call | flops 3221225472 | bytes 10485760 | tf_op jit(solution)/shard_map/local/pallas_call | solution.py:317
  27.3 1.1 all-to-all-done.got
  28.4 0.8 chain.1
  29.1 8.2 %all-to-all-start.1 = ((bf16[32,32,128]{2,1,0:T(8,128)(2,1)}), bf16[32,32,128]{2,1,0:T(8,128)(2,1)S(1)}, u32[]{:S(2)}, u32[]{:S(2)}) async-start(bf16[32,32,128]{2,1,0:T(8,128)(2,1)} %get-tuple-element.30), calls=%async_computation.1 | async-start | bytes 524288 | tf_op jit(solution)/shard_map/all_to_all | solution.py:372
  37.3 7.5 %local.3 = (f32[4,3,1024,128]{3,2,1,0:T(8,128)}, f32[8,128]{1,0:T(8,128)S(1)}) custom-call(s32[1]{0:T(128)} %bitcast.5.target, f32[8,128]{1,0:T(8,128)S(1)} %get-tuple-element.31.after, f32[8,1024]{1,0:T(8,128)} %get-tuple-element.24.after.seg_row, f32[1024,128]{1,0:T(8,128)} %get-tuple-element.25.seg_col, ...), custom_call_target="tpu_custom_call", output_to_operand_aliasing={{0}: (9, {})} | custom-call | flops 3221225472 | bytes 10485760 | tf_op jit(solution)/shard_map/local/pallas_call | solution.py:317
  44.8 2.2 %all-to-all-done.1.states = bf16[32,32,128]{2,1,0:T(8,128)(2,1)S(1)} async-done(((bf16[32,32,128]{2,1,0:T(8,128)(2,1)}), bf16[32,32,128]{2,1,0:T(8,128)(2,1)S(1)}, u32[]{:S(2)}, u32[]{:S(2)}) %all-to-all-start.1) | async-done | bytes 262176 | tf_op jit(solution)/shard_map/all_to_all | solution.py:372
  46.9 0.0 copy-start
  46.9 2.3 %finish.1 = (bf16[3,256,256]{2,1,0:T(8,128)(2,1)}, f32[8,128]{1,0:T(8,128)S(1)}) custom-call(f32[3,256,256]{2,1,0:T(8,128)} %get-tuple-element.26.kept_q.kept_k.kept_v, f32[3,256,256]{2,1,0:T(8,128)} %get-tuple-element.26.kept_q.kept_k.kept_v, f32[3,256,256]{2,1,0:T(8,128)} %get-tuple-element.26.kept_q.kept_k.kept_v, ...), custom_call_target="tpu_custom_call" | custom-call | flops 1 | bytes 1 | tf_op jit(solution)/shard_map/finish/pallas_call | solution.py:381
  49.2 2.9 %collective-permute-start = (bf16[3,256,256]{2,1,0:T(8,128)(2,1)}, bf16[3,256,256]{2,1,0:T(8,128)(2,1)}, u32[]{:S(2)}, u32[]{:S(2)}) collective-permute-start(bf16[3,256,256]{2,1,0:T(8,128)(2,1)} %get-tuple-element.37), channel_id=1, source_target_pairs={{0,4},{1,5},{2,6},{3,7},{4,0},{5,1},{6,2},{7,3},{8,12},{9,13},{10,... | collective-permute-start | bytes 1179656 | tf_op jit(solution)/shard_map/ppermute | solution.py:463
  52.1 0.1 pad_add_fusion.1.targets
  52.2 8.8 %combine.1 = (bf16[3,1024,512]{2,1,0:T(8,128)(2,1)S(1)}, bf16[3,256,256]{2,1,0:T(8,128)(2,1)}, bf16[3,256,512]{2,1,0:T(8,128)(2,1)}) custom-call(s32[2]{0:T(128)S(1)} %pad_add_fusion.1.targets, f32[8,128]{1,0:T(8,128)S(1)} %get-tuple-element.34.after, f32[1024,128]{1,0:T(8,128)} %get-tuple-element.25.seg_col, s32[1,1024]{1,0:T(1,128)} %get-tuple-element.23.dest, ...), custom_call_target="tpu_custom_call" | custom-call | flops 1 | bytes 1 | tf_op jit(solution)/shard_map/combine/pallas_call | solution.py:397
  61.0 0.0 collective-permute-done.refs_0_
  61.0 4.3 %collective-permute-start.7 = (bf16[3,256,512]{2,1,0:T(8,128)(2,1)}, bf16[3,256,512]{2,1,0:T(8,128)(2,1)}, u32[]{:S(2)}, u32[]{:S(2)}) collective-permute-start(bf16[3,256,512]{2,1,0:T(8,128)(2,1)} %get-tuple-element.40), channel_id=1, source_target_pairs={{0,5},{1,4},{2,7},{3,6},{4,1},{5,0},{6,3},{7,2},{8,13},{9,12},{10,... | collective-permute-start | bytes 2359304 | tf_op jit(solution)/shard_map/ppermute | solution.py:463
  65.4 2.5 %collective-permute-start.6 = (bf16[3,256,256]{2,1,0:T(8,128)(2,1)}, bf16[3,256,256]{2,1,0:T(8,128)(2,1)}, u32[]{:S(2)}, u32[]{:S(2)}) collective-permute-start(bf16[3,256,256]{2,1,0:T(8,128)(2,1)} %get-tuple-element.38), channel_id=1, source_target_pairs={{0,4},{1,5},{2,6},{3,7},{4,0},{5,1},{6,2},{7,3},{8,12},{9,13},{10,... | collective-permute-start | bytes 1179656 | tf_op jit(solution)/shard_map/ppermute | solution.py:463
  67.9 0.0 copy-done
  67.9 1.9 %place.8 = bf16[3,256,512]{2,1,0:T(8,128)(2,1)} custom-call(s32[1]{0:T(128)} %bitcast.11.target, s32[1,1024]{1,0:T(1,128)S(1)} %copy-done, bf16[3,1024,512]{2,1,0:T(8,128)(2,1)S(1)} %get-tuple-element.36.grads, bf16[3,256,256]{2,1,0:T(8,128)(2,1)} %collective-permute-done.refs_0_), custom_call_target="tpu_custom_call" | custom-call | flops 1 | bytes 1 | tf_op jit(solution)/shard_map/place/pallas_call | solution.py:452
  69.8 0.4 collective-permute-start.3
  70.2 1.9 %place.9 = bf16[3,256,512]{2,1,0:T(8,128)(2,1)} custom-call(s32[1]{0:T(128)} %bitcast.12.target, s32[1,1024]{1,0:T(1,128)S(1)} %copy-done, bf16[3,1024,512]{2,1,0:T(8,128)(2,1)S(1)} %get-tuple-element.36.grads, bf16[3,256,256]{2,1,0:T(8,128)(2,1)} %collective-permute-done.refs_0_), custom_call_target="tpu_custom_call" | custom-call | flops 1 | bytes 1 | tf_op jit(solution)/shard_map/place/pallas_call | solution.py:452
  72.1 2.3 %collective-permute-start.4 = (bf16[3,256,512]{2,1,0:T(8,128)(2,1)}, bf16[3,256,512]{2,1,0:T(8,128)(2,1)}, u32[]{:S(2)}, u32[]{:S(2)}) collective-permute-start(bf16[3,256,512]{2,1,0:T(8,128)(2,1)} %place.9), channel_id=1, source_target_pairs={{0,6},{1,7},{2,0},{3,1},{4,2},{5,3},{6,4},{7,5},{8,14},{9,15},{10,... | collective-permute-start | bytes 2359304 | tf_op jit(solution)/shard_map/ppermute | solution.py:463
  74.3 1.9 %place.10 = bf16[3,256,512]{2,1,0:T(8,128)(2,1)} custom-call(s32[1]{0:T(128)} %bitcast.10.target, s32[1,1024]{1,0:T(1,128)S(1)} %copy-done, bf16[3,1024,512]{2,1,0:T(8,128)(2,1)S(1)} %get-tuple-element.36.grads, bf16[3,256,256]{2,1,0:T(8,128)(2,1)} %collective-permute-done.refs_0_), custom_call_target="tpu_custom_call" | custom-call | flops 1 | bytes 1 | tf_op jit(solution)/shard_map/place/pallas_call | solution.py:452
  76.2 0.0 collective-permute-start.5
  76.2 1.9 %place.7 = bf16[3,256,512]{2,1,0:T(8,128)(2,1)} custom-call(s32[1]{0:T(128)} %bitcast.7.target, s32[1,1024]{1,0:T(1,128)S(1)} %copy-done, bf16[3,1024,512]{2,1,0:T(8,128)(2,1)S(1)} %get-tuple-element.36.grads, bf16[3,256,256]{2,1,0:T(8,128)(2,1)} %collective-permute-done.refs_0_), custom_call_target="tpu_custom_call" | custom-call | flops 1 | bytes 1 | tf_op jit(solution)/shard_map/place/pallas_call | solution.py:452
  78.1 1.9 %place.6 = bf16[3,256,512]{2,1,0:T(8,128)(2,1)} custom-call(s32[1]{0:T(128)} %bitcast.2.target, s32[1,1024]{1,0:T(1,128)S(1)} %copy-done, bf16[3,1024,512]{2,1,0:T(8,128)(2,1)S(1)} %get-tuple-element.36.grads, bf16[3,256,256]{2,1,0:T(8,128)(2,1)} %collective-permute-done.refs_0_), custom_call_target="tpu_custom_call" | custom-call | flops 1 | bytes 1 | tf_op jit(solution)/shard_map/place/pallas_call | solution.py:452
  80.0 14.5 %collective-permute-done.6.refs_1_ = bf16[3,256,256]{2,1,0:T(8,128)(2,1)} collective-permute-done((bf16[3,256,256]{2,1,0:T(8,128)(2,1)}, bf16[3,256,256]{2,1,0:T(8,128)(2,1)}, u32[]{:S(2)}, u32[]{:S(2)}) %collective-permute-start.6) | collective-permute-done | bytes 393248 | tf_op jit(solution)/shard_map/ppermute | solution.py:463
  94.5 0.0 collective-permute-start.1
  94.5 0.0 collective-permute-done.7.refs_2_
  94.5 3.0 %collective-permute-start.2 = (bf16[3,256,512]{2,1,0:T(8,128)(2,1)}, bf16[3,256,512]{2,1,0:T(8,128)(2,1)}, u32[]{:S(2)}, u32[]{:S(2)}) collective-permute-start(bf16[3,256,512]{2,1,0:T(8,128)(2,1)} %place.7), channel_id=1, source_target_pairs={{0,7},{1,6},{2,1},{3,0},{4,3},{5,2},{6,5},{7,4},{8,15},{9,14},{10,... | collective-permute-start | bytes 2359304 | tf_op jit(solution)/shard_map/ppermute | solution.py:463
  97.5 0.1 pad_add_fusion.sources
  97.6 0.1 pad_add_fusion.3.sources
  97.6 1.9 %place.11.refs_3_ = bf16[3,256,4096]{2,1,0:T(8,128)(2,1)} custom-call(s32[1]{0:T(128)} %bitcast.15.target, s32[1,1024]{1,0:T(1,128)S(1)} %copy-done, bf16[3,1024,512]{2,1,0:T(8,128)(2,1)S(1)} %get-tuple-element.36.grads, bf16[3,256,256]{2,1,0:T(8,128)(2,1)} %collective-permute-done.refs_0_), custom_call_target="tpu_custom_call" | custom-call | flops 1 | bytes 1 | tf_op jit(solution)/shard_map/place/pallas_call | solution.py:439
  99.5 0.1 pad_add_fusion.2.sources
  99.6 2.8 %unpack.3.refs_3_ = bf16[3,256,4096]{2,1,0:T(8,128)(2,1)} custom-call(s32[3]{0:T(128)S(1)} %pad_add_fusion.3.sources, bf16[3,256,256]{2,1,0:T(8,128)(2,1)} %collective-permute-done.refs_0_, bf16[3,256,256]{2,1,0:T(8,128)(2,1)} %collective-permute-done.6.refs_1_, bf16[3,256,512]{2,1,0:T(8,128)(2,1)} %collective-permute-done.7.refs_2_, ...), custom_call_target="tpu_custom_call", output_to_operand_aliasing={{}: (4, {})} | custom-call | flops 1 | bytes 1 | tf_op jit(solution)/shard_map/unpack/pallas_call | solution.py:480
  102.4 6.8 %collective-permute-done.3.refs_0_ = bf16[3,256,512]{2,1,0:T(8,128)(2,1)} collective-permute-done((bf16[3,256,512]{2,1,0:T(8,128)(2,1)}, bf16[3,256,512]{2,1,0:T(8,128)(2,1)}, u32[]{:S(2)}, u32[]{:S(2)}) %collective-permute-start.3) | collective-permute-done | bytes 786464 | tf_op jit(solution)/shard_map/ppermute | solution.py:463
  109.3 0.7 collective-permute-done.4.refs_1_
  109.9 0.0 collective-permute-done.5.refs_2_
  109.9 3.1 %unpack.4.refs_2_ = bf16[3,256,4096]{2,1,0:T(8,128)(2,1)} custom-call(s32[3]{0:T(128)S(1)} %pad_add_fusion.2.sources, bf16[3,256,512]{2,1,0:T(8,128)(2,1)} %collective-permute-done.3.refs_0_, bf16[3,256,512]{2,1,0:T(8,128)(2,1)} %collective-permute-done.4.refs_1_, ...), custom_call_target="tpu_custom_call", output_to_operand_aliasing={{}: (4, {})} | custom-call | flops 1 | bytes 1 | tf_op jit(solution)/shard_map/unpack/pallas_call | solution.py:480
  113.1 13.1 %collective-permute-done.1.refs_0_ = bf16[3,256,512]{2,1,0:T(8,128)(2,1)} collective-permute-done((bf16[3,256,512]{2,1,0:T(8,128)(2,1)}, bf16[3,256,512]{2,1,0:T(8,128)(2,1)}, u32[]{:S(2)}, u32[]{:S(2)}) %collective-permute-start.1) | collective-permute-done | bytes 786464 | tf_op jit(solution)/shard_map/ppermute | solution.py:463
  126.1 0.0 collective-permute-done.2.refs_1_
  126.1 2.8 %unpack.5 = bf16[3,256,4096]{2,1,0:T(8,128)(2,1)} custom-call(s32[2]{0:T(128)S(1)} %pad_add_fusion.sources, bf16[3,256,512]{2,1,0:T(8,128)(2,1)} %collective-permute-done.1.refs_0_, bf16[3,256,512]{2,1,0:T(8,128)(2,1)} %collective-permute-done.2.refs_1_, bf16[3,256,4096]{2,1,0:T(8,128)(2,1)} %unpack.4.refs_2_), custom_call_target="tpu_custom_call", output_to_operand_aliasing={{}: (3, {})} | custom-call | flops 1 | bytes 1 | tf_op jit(solution)/shard_map/unpack/pallas_call | solution.py:480
Async XLA Ops:
  4.8 23.5 %all-to-all-start = ((bf16[32,48,128]{2,1,0:T(8,128)(2,1)}), bf16[32,48,128]{2,1,0:T(8,128)(2,1)S(1)}, u32[]{:S(2)}, u32[]{:S(2)}) async-start(bf16[32,48,128]{2,1,0:T(8,128)(2,1)} %get-tuple-element.28), calls=%async_computation | async-start | bytes 786432 | tf_op jit(solution)/shard_map/all_to_all | solution.py:289
  29.1 17.8 %all-to-all-start.1 = ((bf16[32,32,128]{2,1,0:T(8,128)(2,1)}), bf16[32,32,128]{2,1,0:T(8,128)(2,1)S(1)}, u32[]{:S(2)}, u32[]{:S(2)}) async-start(bf16[32,32,128]{2,1,0:T(8,128)(2,1)} %get-tuple-element.30), calls=%async_computation.1 | async-start | bytes 524288 | tf_op jit(solution)/shard_map/all_to_all | solution.py:372
  46.9 20.9 %copy-start = (s32[1,1024]{1,0:T(1,128)S(1)}, s32[1,1024]{1,0:T(1,128)}, u32[]{:S(2)}) copy-start(s32[1,1024]{1,0:T(1,128)} %get-tuple-element.23.dest) | copy-start | bytes 12292
  49.2 11.8 %collective-permute-start = (bf16[3,256,256]{2,1,0:T(8,128)(2,1)}, bf16[3,256,256]{2,1,0:T(8,128)(2,1)}, u32[]{:S(2)}, u32[]{:S(2)}) collective-permute-start(bf16[3,256,256]{2,1,0:T(8,128)(2,1)} %get-tuple-element.37), channel_id=1, source_target_pairs={{0,4},{1,5},{2,6},{3,7},{4,0},{5,1},{6,2},{7,3},{8,12},{9,13},{10,... | collective-permute-start | bytes 1179656 | tf_op jit(solution)/shard_map/ppermute | solution.py:463
  61.0 33.5 %collective-permute-start.7 = (bf16[3,256,512]{2,1,0:T(8,128)(2,1)}, bf16[3,256,512]{2,1,0:T(8,128)(2,1)}, u32[]{:S(2)}, u32[]{:S(2)}) collective-permute-start(bf16[3,256,512]{2,1,0:T(8,128)(2,1)} %get-tuple-element.40), channel_id=1, source_target_pairs={{0,5},{1,4},{2,7},{3,6},{4,1},{5,0},{6,3},{7,2},{8,13},{9,12},{10,... | collective-permute-start | bytes 2359304 | tf_op jit(solution)/shard_map/ppermute | solution.py:463
  65.4 29.1 %collective-permute-start.6 = (bf16[3,256,256]{2,1,0:T(8,128)(2,1)}, bf16[3,256,256]{2,1,0:T(8,128)(2,1)}, u32[]{:S(2)}, u32[]{:S(2)}) collective-permute-start(bf16[3,256,256]{2,1,0:T(8,128)(2,1)} %get-tuple-element.38), channel_id=1, source_target_pairs={{0,4},{1,5},{2,6},{3,7},{4,0},{5,1},{6,2},{7,3},{8,12},{9,13},{10,... | collective-permute-start | bytes 1179656 | tf_op jit(solution)/shard_map/ppermute | solution.py:463
  69.8 39.5 %collective-permute-start.3 = (bf16[3,256,512]{2,1,0:T(8,128)(2,1)}, bf16[3,256,512]{2,1,0:T(8,128)(2,1)}, u32[]{:S(2)}, u32[]{:S(2)}) collective-permute-start(bf16[3,256,512]{2,1,0:T(8,128)(2,1)} %place.8), channel_id=1, source_target_pairs={{0,2},{1,3},{2,4},{3,5},{4,6},{5,7},{6,0},{7,1},{8,10},{9,11},{10,... | collective-permute-start | bytes 2359304 | tf_op jit(solution)/shard_map/ppermute | solution.py:463
  72.1 37.9 %collective-permute-start.4 = (bf16[3,256,512]{2,1,0:T(8,128)(2,1)}, bf16[3,256,512]{2,1,0:T(8,128)(2,1)}, u32[]{:S(2)}, u32[]{:S(2)}) collective-permute-start(bf16[3,256,512]{2,1,0:T(8,128)(2,1)} %place.9), channel_id=1, source_target_pairs={{0,6},{1,7},{2,0},{3,1},{4,2},{5,3},{6,4},{7,5},{8,14},{9,15},{10,... | collective-permute-start | bytes 2359304 | tf_op jit(solution)/shard_map/ppermute | solution.py:463
  76.2 33.7 %collective-permute-start.5 = (bf16[3,256,512]{2,1,0:T(8,128)(2,1)}, bf16[3,256,512]{2,1,0:T(8,128)(2,1)}, u32[]{:S(2)}, u32[]{:S(2)}) collective-permute-start(bf16[3,256,512]{2,1,0:T(8,128)(2,1)} %place.10), channel_id=1, source_target_pairs={{0,1},{1,0},{2,3},{3,2},{4,5},{5,4},{6,7},{7,6},{8,9},{9,8},{10,11... | collective-permute-start | bytes 2359304 | tf_op jit(solution)/shard_map/ppermute | solution.py:463
  94.5 31.6 %collective-permute-start.1 = (bf16[3,256,512]{2,1,0:T(8,128)(2,1)}, bf16[3,256,512]{2,1,0:T(8,128)(2,1)}, u32[]{:S(2)}, u32[]{:S(2)}) collective-permute-start(bf16[3,256,512]{2,1,0:T(8,128)(2,1)} %place.6), channel_id=1, source_target_pairs={{0,3},{1,2},{2,5},{3,4},{4,7},{5,6},{6,1},{7,0},{8,11},{9,10},{10,... | collective-permute-start | bytes 2359304 | tf_op jit(solution)/shard_map/ppermute | solution.py:463
  94.5 31.6 %collective-permute-start.2 = (bf16[3,256,512]{2,1,0:T(8,128)(2,1)}, bf16[3,256,512]{2,1,0:T(8,128)(2,1)}, u32[]{:S(2)}, u32[]{:S(2)}) collective-permute-start(bf16[3,256,512]{2,1,0:T(8,128)(2,1)} %place.7), channel_id=1, source_target_pairs={{0,7},{1,6},{2,1},{3,0},{4,3},{5,2},{6,5},{7,4},{8,15},{9,14},{10,... | collective-permute-start | bytes 2359304 | tf_op jit(solution)/shard_map/ppermute | solution.py:463

commit v5 on v4

--- a/solution.py
+++ b/solution.py
@@ -31,7 +31,9 @@
     )
 
 
-def states_body(count, capacity, starts, owners, q, k, v, g, pay, seg_row, seg_col, dest):
+def states_body(
+    count, capacity, starts, owners, q, k, v, g, pay, seg_row, seg_col, dest, fwd, bwd
+):
     span = starts.shape[1]
 
     @pl.when(pl.program_id(0) == 0)
@@ -61,18 +63,33 @@
             dest[:, at : at + HD] = owner[:, at : at + HD] * capacity + slot.astype(jnp.int32)
             seg_col[at : at + HD, :] = jnp.broadcast_to(sums[count : count + 1], (HD, HD)).T
 
-    segment = seg_col[...]
-    total = segment[span - 1 :, :]
+        fwd[...] = jnp.zeros_like(fwd)
+        bwd[...] = jnp.zeros_like(bwd)
+
+    step = pl.program_id(0)
+    size = q.shape[0]
+    segment = seg_col[pl.ds(pl.multiple_of(step * size, size), size), :]
+    total = seg_col[span - 1 :, :]
     first = (segment == 0.0).astype(F32).astype(BF16)
     last = (segment == total).astype(F32).astype(BF16)
-    pieces = pay.shape[0]
-    part = HD // pieces
-    fwd = dot_tn(k[...] * last, v[...]).astype(BF16)
-    bwd = dot_tn(q[...] * first, g[...]).astype(BF16)
-    pay[:, :part, :] = fwd.reshape(pieces, part, HD)
-    pay[:, part : 2 * part, :] = bwd.reshape(pieces, part, HD)
-    keep = (total == 0.0).astype(F32)
-    pay[:, 2 * part :, :] = jnp.broadcast_to(keep[None], (pieces, 16, HD)).astype(BF16)
+    heads = fwd.shape[0]
+    for head in range(heads):
+        own = slice(head * HD, (head + 1) * HD)
+        fwd[head] += dot_tn(k[:, own] * last, v[:, own])
+        bwd[head] += dot_tn(q[:, own] * first, g[:, own])
+
+    @pl.when(step == pl.num_programs(0) - 1)
+    def _():
+        pieces = pay.shape[0] // heads
+        part = HD // pieces
+        for head in range(heads):
+            rows = slice(head * pieces, (head + 1) * pieces)
+            pay[rows, :part, :] = fwd[head].astype(BF16).reshape(pieces, part, HD)
+            pay[rows, part : 2 * part, :] = bwd[head].astype(BF16).reshape(pieces, part, HD)
+        keep = (total == 0.0).astype(F32)
+        pay[:, 2 * part :, :] = jnp.broadcast_to(
+            keep[None], (pay.shape[0], pay.shape[1] - 2 * part, HD)
+        ).astype(BF16)
 
 
 def chain_body(count, part, got, after, out, token):
@@ -235,16 +252,24 @@
     held = refs[many + 4 :]
     loads, stores = [], []
     for turn in range(many):
-        loads.append(pltpu.make_async_copy(refs[turn], held[turn], sems.at[turn]))
-        loads[-1].start()
+        for kind in range(3):
+            loads.append(
+                pltpu.make_async_copy(
+                    refs[turn].at[kind], held[turn].at[kind], sems.at[turn, kind]
+                )
+            )
+            loads[-1].start()
     for turn, lo in enumerate(starts):
-        loads[turn].wait()
         width = held[turn].shape[2]
         cols = pl.ds(pl.multiple_of(sources[turn] * feats + lo, HD), width)
-        stores.append(
-            pltpu.make_async_copy(held[turn], out.at[:, :, cols], out_sems.at[turn])
-        )
-        stores[-1].start()
+        for kind in range(3):
+            loads[turn * 3 + kind].wait()
+            stores.append(
+                pltpu.make_async_copy(
+                    held[turn].at[kind], out.at[kind, :, cols], out_sems.at[turn, kind]
+                )
+            )
+            stores[-1].start()
     for store in stores:
         store.wait()
 
@@ -268,20 +293,22 @@
 
     payload, seg_row, seg_col, dest = pl.pallas_call(
         functools.partial(states_body, count, capacity),
-        grid=(heads,),
-        in_specs=[full(1, span), full(1, span)] + [by_head] * 4,
+        grid=(span // TILE,),
+        in_specs=[full(1, span), full(1, span)]
+        + [pl.BlockSpec((TILE, feats), lambda i: (i, 0))] * 4,
         out_specs=[
-            pl.BlockSpec((pieces, 2 * part + 16, HD), lambda i: (i, 0, 0)),
+            full(n_seq, 2 * part + 8, HD),
             full(8, span),
             full(span, HD),
             full(1, span),
         ],
         out_shape=[
-            jax.ShapeDtypeStruct((n_seq, 2 * part + 16, HD), BF16),
+            jax.ShapeDtypeStruct((n_seq, 2 * part + 8, HD), BF16),
             jax.ShapeDtypeStruct((8, span), F32),
             jax.ShapeDtypeStruct((span, HD), F32),
             jax.ShapeDtypeStruct((1, span), jnp.int32),
         ],
+        scratch_shapes=[pltpu.VMEM((heads, HD, HD), F32)] * 2,
         compiler_params=params(1, 60),
         name="states",
     )(starts_row, owners_row, *in_hbm)
@@ -483,8 +510,8 @@
             out_specs=pl.BlockSpec(memory_space=pl.ANY),
             out_shape=jax.ShapeDtypeStruct((3, capacity, count * feats), BF16),
             scratch_shapes=[
-                pltpu.SemaphoreType.DMA((many,)),
-                pltpu.SemaphoreType.DMA((many,)),
+                pltpu.SemaphoreType.DMA((many, 3)),
+                pltpu.SemaphoreType.DMA((many, 3)),
             ]
             + [pltpu.VMEM(one.shape, BF16) for one in received[lo:hi]],
             input_output_aliases={many + 1: 0},

time: 130 us -> 130 us (level)
  transfers between devices with their start and end apart: 10 -> 10, of which waited for: 6 -> 5; matrix products, arithmetic and copies ran while one was open for 0% -> 0% of each run, Pallas kernels for 34% -> 34%
where the time goes in v5:
time: 130 us; the launch traced here: 129 us
  Pallas kernels  54.7 us (42%)
  waiting for transfers between devices  37.3 us (29%)
  starting transfers between devices  36.5 us (28%)
    ppermute x8, waiting for transfers between devices, sent(): lax.ppermute(chunk, 'head', [(index, moved(index, hop, 1)) for index in r...  35.1 us
    pallas_call x2, Pallas kernels, local_half(): pl.pallas_call(functools.partial(local_body, ahead), grid_spec=pltpu.Pref...  17.9 us
    ppermute x8, starting transfers between devices, sent(): lax.ppermute(chunk, 'head', [(index, moved(index, hop, 1)) for index in r...  15.4 us
    all_to_all x1, starting transfers between devices, shards(): gathered = lax.all_to_all(payload, 'seq', 0, 0, tiled=True)  11.9 us
    pallas_call x5, Pallas kernels, place(): pl.pallas_call(functools.partial(place_body, lo), in_specs=[smem] + [whol...  9.43 us
    all_to_all x1, starting transfers between devices, shards(): states = lax.all_to_all(chained, 'seq', 0, 0, tiled=True)  9.22 us
    pallas_call x1, Pallas kernels, combine(): pl.pallas_call(functools.partial(combine_body, part, half), grid_spec=plt...  8.82 us
    pallas_call x3, Pallas kernels, shards(): pl.pallas_call(functools.partial(unpack_body, feats, [start for _, start...  8.63 us
  transfers between devices with their start and end apart: 10, of which 5 were waited for; matrix products, arithmetic and copies ran while one was open for 0% of the time, Pallas kernels for 34%

profile of v5, /device:TPU:1, one launch (start us, length us, event | category | flops | bytes accessed | tf_op | source)
XLA Modules:
  0.0 129.1 jit_solution(14422303963533239532)
XLA Ops:
  0.0 4.9 %states.1 = (bf16[32,40,128]{2,1,0:T(8,128)(2,1)}, f32[8,1024]{1,0:T(8,128)}, f32[1024,128]{1,0:T(8,128)}, s32[1,1024]{1,0:T(1,128)}) custom-call(s32[1,1024]{1,0:T(1,128)} %bitcast.17, s32[1,1024]{1,0:T(1,128)} %bitcast.18, bf16[1024,512]{1,0:T(8,128)(2,1)} %q.5, bf16[1024,512]{1,0:T(8,128)(2,1)} %k.7, bf16[1024,512]{1,0:T(8,128)(2,1)} %v.7, ...), custom_call_target="tpu_custom_call" | custom-call | tf_op jit(solution)/shard_map/states/pallas_call | solution.py:294
  4.9 11.9 %all-to-all-start = ((bf16[32,40,128]{2,1,0:T(8,128)(2,1)}), bf16[32,40,128]{2,1,0:T(8,128)(2,1)S(1)}, u32[]{:S(2)}, u32[]{:S(2)}) async-start(bf16[32,40,128]{2,1,0:T(8,128)(2,1)} %get-tuple-element.28), calls=%async_computation | async-start | bytes 655360 | tf_op jit(solution)/shard_map/all_to_all | solution.py:316
  16.9 10.5 %local.2 = (f32[4,3,1024,128]{3,2,1,0:T(8,128)}, f32[8,128]{1,0:T(8,128)S(1)}, f32[3,256,256]{2,1,0:T(8,128)}, bf16[3,256,256]{2,1,0:T(8,128)(2,1)}) custom-call(s32[1]{0:T(128)} %bitcast.5.target, f32[8,1024]{1,0:T(8,128)} %get-tuple-element.24.after.seg_row, f32[8,1024]{1,0:T(8,128)} %get-tuple-element.24.after.seg_row, ...), custom_call_target="tpu_custom_call" | custom-call | flops 3221225472 | bytes 10485760 | tf_op jit(solution)/shard_map/local/pallas_call | solution.py:344
  27.4 0.0 all-to-all-done.got
  27.4 0.8 chain.1
  28.2 9.2 %all-to-all-start.1 = ((bf16[32,32,128]{2,1,0:T(8,128)(2,1)}), bf16[32,32,128]{2,1,0:T(8,128)(2,1)S(1)}, u32[]{:S(2)}, u32[]{:S(2)}) async-start(bf16[32,32,128]{2,1,0:T(8,128)(2,1)} %get-tuple-element.30), calls=%async_computation.1 | async-start | bytes 524288 | tf_op jit(solution)/shard_map/all_to_all | solution.py:399
  37.4 7.5 %local.3 = (f32[4,3,1024,128]{3,2,1,0:T(8,128)}, f32[8,128]{1,0:T(8,128)S(1)}) custom-call(s32[1]{0:T(128)} %bitcast.5.target, f32[8,128]{1,0:T(8,128)S(1)} %get-tuple-element.31.after, f32[8,1024]{1,0:T(8,128)} %get-tuple-element.24.after.seg_row, f32[1024,128]{1,0:T(8,128)} %get-tuple-element.25.seg_col, ...), custom_call_target="tpu_custom_call", output_to_operand_aliasing={{0}: (9, {})} | custom-call | flops 3221225472 | bytes 10485760 | tf_op jit(solution)/shard_map/local/pallas_call | solution.py:344
  44.9 2.2 %all-to-all-done.1.states = bf16[32,32,128]{2,1,0:T(8,128)(2,1)S(1)} async-done(((bf16[32,32,128]{2,1,0:T(8,128)(2,1)}), bf16[32,32,128]{2,1,0:T(8,128)(2,1)S(1)}, u32[]{:S(2)}, u32[]{:S(2)}) %all-to-all-start.1) | async-done | bytes 262176 | tf_op jit(solution)/shard_map/all_to_all | solution.py:399
  47.1 0.0 copy-start
  47.1 2.3 %finish.1 = (bf16[3,256,256]{2,1,0:T(8,128)(2,1)}, f32[8,128]{1,0:T(8,128)S(1)}) custom-call(f32[3,256,256]{2,1,0:T(8,128)} %get-tuple-element.26.kept_q.kept_k.kept_v, f32[3,256,256]{2,1,0:T(8,128)} %get-tuple-element.26.kept_q.kept_k.kept_v, f32[3,256,256]{2,1,0:T(8,128)} %get-tuple-element.26.kept_q.kept_k.kept_v, ...), custom_call_target="tpu_custom_call" | custom-call | flops 1 | bytes 1 | tf_op jit(solution)/shard_map/finish/pallas_call | solution.py:408
  49.4 2.9 %collective-permute-start = (bf16[3,256,256]{2,1,0:T(8,128)(2,1)}, bf16[3,256,256]{2,1,0:T(8,128)(2,1)}, u32[]{:S(2)}, u32[]{:S(2)}) collective-permute-start(bf16[3,256,256]{2,1,0:T(8,128)(2,1)} %get-tuple-element.37), channel_id=1, source_target_pairs={{0,4},{1,5},{2,6},{3,7},{4,0},{5,1},{6,2},{7,3},{8,12},{9,13},{10,... | collective-permute-start | bytes 1179656 | tf_op jit(solution)/shard_map/ppermute | solution.py:490
  52.3 0.1 pad_add_fusion.1.targets
  52.3 8.8 %combine.1 = (bf16[3,1024,512]{2,1,0:T(8,128)(2,1)S(1)}, bf16[3,256,256]{2,1,0:T(8,128)(2,1)}, bf16[3,256,512]{2,1,0:T(8,128)(2,1)}) custom-call(s32[2]{0:T(128)S(1)} %pad_add_fusion.1.targets, f32[8,128]{1,0:T(8,128)S(1)} %get-tuple-element.34.after, f32[1024,128]{1,0:T(8,128)} %get-tuple-element.25.seg_col, s32[1,1024]{1,0:T(1,128)} %get-tuple-element.23.dest, ...), custom_call_target="tpu_custom_call" | custom-call | flops 1 | bytes 1 | tf_op jit(solution)/shard_map/combine/pallas_call | solution.py:424
  61.2 0.0 collective-permute-done.refs_0_
  61.2 4.3 %collective-permute-start.7 = (bf16[3,256,512]{2,1,0:T(8,128)(2,1)}, bf16[3,256,512]{2,1,0:T(8,128)(2,1)}, u32[]{:S(2)}, u32[]{:S(2)}) collective-permute-start(bf16[3,256,512]{2,1,0:T(8,128)(2,1)} %get-tuple-element.40), channel_id=1, source_target_pairs={{0,5},{1,4},{2,7},{3,6},{4,1},{5,0},{6,3},{7,2},{8,13},{9,12},{10,... | collective-permute-start | bytes 2359304 | tf_op jit(solution)/shard_map/ppermute | solution.py:490
  65.5 2.5 %collective-permute-start.6 = (bf16[3,256,256]{2,1,0:T(8,128)(2,1)}, bf16[3,256,256]{2,1,0:T(8,128)(2,1)}, u32[]{:S(2)}, u32[]{:S(2)}) collective-permute-start(bf16[3,256,256]{2,1,0:T(8,128)(2,1)} %get-tuple-element.38), channel_id=1, source_target_pairs={{0,4},{1,5},{2,6},{3,7},{4,0},{5,1},{6,2},{7,3},{8,12},{9,13},{10,... | collective-permute-start | bytes 1179656 | tf_op jit(solution)/shard_map/ppermute | solution.py:490
  68.0 0.0 copy-done
  68.0 1.9 %place.8 = bf16[3,256,512]{2,1,0:T(8,128)(2,1)} custom-call(s32[1]{0:T(128)} %bitcast.11.target, s32[1,1024]{1,0:T(1,128)S(1)} %copy-done, bf16[3,1024,512]{2,1,0:T(8,128)(2,1)S(1)} %get-tuple-element.36.grads, bf16[3,256,256]{2,1,0:T(8,128)(2,1)} %collective-permute-done.refs_0_), custom_call_target="tpu_custom_call" | custom-call | flops 1 | bytes 1 | tf_op jit(solution)/shard_map/place/pallas_call | solution.py:479
  69.9 0.4 collective-permute-start.3
  70.3 1.9 %place.9 = bf16[3,256,512]{2,1,0:T(8,128)(2,1)} custom-call(s32[1]{0:T(128)} %bitcast.12.target, s32[1,1024]{1,0:T(1,128)S(1)} %copy-done, bf16[3,1024,512]{2,1,0:T(8,128)(2,1)S(1)} %get-tuple-element.36.grads, bf16[3,256,256]{2,1,0:T(8,128)(2,1)} %collective-permute-done.refs_0_), custom_call_target="tpu_custom_call" | custom-call | flops 1 | bytes 1 | tf_op jit(solution)/shard_map/place/pallas_call | solution.py:479
  72.2 2.3 %collective-permute-start.4 = (bf16[3,256,512]{2,1,0:T(8,128)(2,1)}, bf16[3,256,512]{2,1,0:T(8,128)(2,1)}, u32[]{:S(2)}, u32[]{:S(2)}) collective-permute-start(bf16[3,256,512]{2,1,0:T(8,128)(2,1)} %place.9), channel_id=1, source_target_pairs={{0,6},{1,7},{2,0},{3,1},{4,2},{5,3},{6,4},{7,5},{8,14},{9,15},{10,... | collective-permute-start | bytes 2359304 | tf_op jit(solution)/shard_map/ppermute | solution.py:490
  74.5 1.9 %place.10 = bf16[3,256,512]{2,1,0:T(8,128)(2,1)} custom-call(s32[1]{0:T(128)} %bitcast.10.target, s32[1,1024]{1,0:T(1,128)S(1)} %copy-done, bf16[3,1024,512]{2,1,0:T(8,128)(2,1)S(1)} %get-tuple-element.36.grads, bf16[3,256,256]{2,1,0:T(8,128)(2,1)} %collective-permute-done.refs_0_), custom_call_target="tpu_custom_call" | custom-call | flops 1 | bytes 1 | tf_op jit(solution)/shard_map/place/pallas_call | solution.py:479
  76.3 0.0 collective-permute-start.5
  76.3 1.9 %place.7 = bf16[3,256,512]{2,1,0:T(8,128)(2,1)} custom-call(s32[1]{0:T(128)} %bitcast.7.target, s32[1,1024]{1,0:T(1,128)S(1)} %copy-done, bf16[3,1024,512]{2,1,0:T(8,128)(2,1)S(1)} %get-tuple-element.36.grads, bf16[3,256,256]{2,1,0:T(8,128)(2,1)} %collective-permute-done.refs_0_), custom_call_target="tpu_custom_call" | custom-call | flops 1 | bytes 1 | tf_op jit(solution)/shard_map/place/pallas_call | solution.py:479
  78.2 1.9 %place.6 = bf16[3,256,512]{2,1,0:T(8,128)(2,1)} custom-call(s32[1]{0:T(128)} %bitcast.2.target, s32[1,1024]{1,0:T(1,128)S(1)} %copy-done, bf16[3,1024,512]{2,1,0:T(8,128)(2,1)S(1)} %get-tuple-element.36.grads, bf16[3,256,256]{2,1,0:T(8,128)(2,1)} %collective-permute-done.refs_0_), custom_call_target="tpu_custom_call" | custom-call | flops 1 | bytes 1 | tf_op jit(solution)/shard_map/place/pallas_call | solution.py:479
  80.1 14.5 %collective-permute-done.6.refs_1_ = bf16[3,256,256]{2,1,0:T(8,128)(2,1)} collective-permute-done((bf16[3,256,256]{2,1,0:T(8,128)(2,1)}, bf16[3,256,256]{2,1,0:T(8,128)(2,1)}, u32[]{:S(2)}, u32[]{:S(2)}) %collective-permute-start.6) | collective-permute-done | bytes 393248 | tf_op jit(solution)/shard_map/ppermute | solution.py:490
  94.7 0.0 collective-permute-start.1
  94.7 0.0 collective-permute-done.7.refs_2_
  94.7 3.0 %collective-permute-start.2 = (bf16[3,256,512]{2,1,0:T(8,128)(2,1)}, bf16[3,256,512]{2,1,0:T(8,128)(2,1)}, u32[]{:S(2)}, u32[]{:S(2)}) collective-permute-start(bf16[3,256,512]{2,1,0:T(8,128)(2,1)} %place.7), channel_id=1, source_target_pairs={{0,7},{1,6},{2,1},{3,0},{4,3},{5,2},{6,5},{7,4},{8,15},{9,14},{10,... | collective-permute-start | bytes 2359304 | tf_op jit(solution)/shard_map/ppermute | solution.py:490
  97.6 0.1 pad_add_fusion.sources
  97.7 0.1 pad_add_fusion.3.sources
  97.8 1.9 %place.11.refs_3_ = bf16[3,256,4096]{2,1,0:T(8,128)(2,1)} custom-call(s32[1]{0:T(128)} %bitcast.15.target, s32[1,1024]{1,0:T(1,128)S(1)} %copy-done, bf16[3,1024,512]{2,1,0:T(8,128)(2,1)S(1)} %get-tuple-element.36.grads, bf16[3,256,256]{2,1,0:T(8,128)(2,1)} %collective-permute-done.refs_0_), custom_call_target="tpu_custom_call" | custom-call | flops 1 | bytes 1 | tf_op jit(solution)/shard_map/place/pallas_call | solution.py:466
  99.7 0.1 pad_add_fusion.2.sources
  99.7 2.9 %unpack.3.refs_3_ = bf16[3,256,4096]{2,1,0:T(8,128)(2,1)} custom-call(s32[3]{0:T(128)S(1)} %pad_add_fusion.3.sources, bf16[3,256,256]{2,1,0:T(8,128)(2,1)} %collective-permute-done.refs_0_, bf16[3,256,256]{2,1,0:T(8,128)(2,1)} %collective-permute-done.6.refs_1_, bf16[3,256,512]{2,1,0:T(8,128)(2,1)} %collective-permute-done.7.refs_2_, ...), custom_call_target="tpu_custom_call", output_to_operand_aliasing={{}: (4, {})} | custom-call | flops 1 | bytes 1 | tf_op jit(solution)/shard_map/unpack/pallas_call | solution.py:507
  102.6 6.8 %collective-permute-done.3.refs_0_ = bf16[3,256,512]{2,1,0:T(8,128)(2,1)} collective-permute-done((bf16[3,256,512]{2,1,0:T(8,128)(2,1)}, bf16[3,256,512]{2,1,0:T(8,128)(2,1)}, u32[]{:S(2)}, u32[]{:S(2)}) %collective-permute-start.3) | collective-permute-done | bytes 786464 | tf_op jit(solution)/shard_map/ppermute | solution.py:490
  109.4 0.7 collective-permute-done.4.refs_1_
  110.1 0.0 collective-permute-done.5.refs_2_
  110.1 3.0 %unpack.4.refs_2_ = bf16[3,256,4096]{2,1,0:T(8,128)(2,1)} custom-call(s32[3]{0:T(128)S(1)} %pad_add_fusion.2.sources, bf16[3,256,512]{2,1,0:T(8,128)(2,1)} %collective-permute-done.3.refs_0_, bf16[3,256,512]{2,1,0:T(8,128)(2,1)} %collective-permute-done.4.refs_1_, ...), custom_call_target="tpu_custom_call", output_to_operand_aliasing={{}: (4, {})} | custom-call | flops 1 | bytes 1 | tf_op jit(solution)/shard_map/unpack/pallas_call | solution.py:507
  113.1 13.1 %collective-permute-done.1.refs_0_ = bf16[3,256,512]{2,1,0:T(8,128)(2,1)} collective-permute-done((bf16[3,256,512]{2,1,0:T(8,128)(2,1)}, bf16[3,256,512]{2,1,0:T(8,128)(2,1)}, u32[]{:S(2)}, u32[]{:S(2)}) %collective-permute-start.1) | collective-permute-done | bytes 786464 | tf_op jit(solution)/shard_map/ppermute | solution.py:490
  126.2 0.0 collective-permute-done.2.refs_1_
  126.2 2.7 %unpack.5 = bf16[3,256,4096]{2,1,0:T(8,128)(2,1)} custom-call(s32[2]{0:T(128)S(1)} %pad_add_fusion.sources, bf16[3,256,512]{2,1,0:T(8,128)(2,1)} %collective-permute-done.1.refs_0_, bf16[3,256,512]{2,1,0:T(8,128)(2,1)} %collective-permute-done.2.refs_1_, bf16[3,256,4096]{2,1,0:T(8,128)(2,1)} %unpack.4.refs_2_), custom_call_target="tpu_custom_call", output_to_operand_aliasing={{}: (3, {})} | custom-call | flops 1 | bytes 1 | tf_op jit(solution)/shard_map/unpack/pallas_call | solution.py:507
Async XLA Ops:
  4.9 22.4 %all-to-all-start = ((bf16[32,40,128]{2,1,0:T(8,128)(2,1)}), bf16[32,40,128]{2,1,0:T(8,128)(2,1)S(1)}, u32[]{:S(2)}, u32[]{:S(2)}) async-start(bf16[32,40,128]{2,1,0:T(8,128)(2,1)} %get-tuple-element.28), calls=%async_computation | async-start | bytes 655360 | tf_op jit(solution)/shard_map/all_to_all | solution.py:316
  28.2 18.9 %all-to-all-start.1 = ((bf16[32,32,128]{2,1,0:T(8,128)(2,1)}), bf16[32,32,128]{2,1,0:T(8,128)(2,1)S(1)}, u32[]{:S(2)}, u32[]{:S(2)}) async-start(bf16[32,32,128]{2,1,0:T(8,128)(2,1)} %get-tuple-element.30), calls=%async_computation.1 | async-start | bytes 524288 | tf_op jit(solution)/shard_map/all_to_all | solution.py:399
  47.1 20.9 %copy-start = (s32[1,1024]{1,0:T(1,128)S(1)}, s32[1,1024]{1,0:T(1,128)}, u32[]{:S(2)}) copy-start(s32[1,1024]{1,0:T(1,128)} %get-tuple-element.23.dest) | copy-start | bytes 12292
  49.4 11.8 %collective-permute-start = (bf16[3,256,256]{2,1,0:T(8,128)(2,1)}, bf16[3,256,256]{2,1,0:T(8,128)(2,1)}, u32[]{:S(2)}, u32[]{:S(2)}) collective-permute-start(bf16[3,256,256]{2,1,0:T(8,128)(2,1)} %get-tuple-element.37), channel_id=1, source_target_pairs={{0,4},{1,5},{2,6},{3,7},{4,0},{5,1},{6,2},{7,3},{8,12},{9,13},{10,... | collective-permute-start | bytes 1179656 | tf_op jit(solution)/shard_map/ppermute | solution.py:490
  61.2 33.5 %collective-permute-start.7 = (bf16[3,256,512]{2,1,0:T(8,128)(2,1)}, bf16[3,256,512]{2,1,0:T(8,128)(2,1)}, u32[]{:S(2)}, u32[]{:S(2)}) collective-permute-start(bf16[3,256,512]{2,1,0:T(8,128)(2,1)} %get-tuple-element.40), channel_id=1, source_target_pairs={{0,5},{1,4},{2,7},{3,6},{4,1},{5,0},{6,3},{7,2},{8,13},{9,12},{10,... | collective-permute-start | bytes 2359304 | tf_op jit(solution)/shard_map/ppermute | solution.py:490
  65.5 29.2 %collective-permute-start.6 = (bf16[3,256,256]{2,1,0:T(8,128)(2,1)}, bf16[3,256,256]{2,1,0:T(8,128)(2,1)}, u32[]{:S(2)}, u32[]{:S(2)}) collective-permute-start(bf16[3,256,256]{2,1,0:T(8,128)(2,1)} %get-tuple-element.38), channel_id=1, source_target_pairs={{0,4},{1,5},{2,6},{3,7},{4,0},{5,1},{6,2},{7,3},{8,12},{9,13},{10,... | collective-permute-start | bytes 1179656 | tf_op jit(solution)/shard_map/ppermute | solution.py:490
  69.9 39.5 %collective-permute-start.3 = (bf16[3,256,512]{2,1,0:T(8,128)(2,1)}, bf16[3,256,512]{2,1,0:T(8,128)(2,1)}, u32[]{:S(2)}, u32[]{:S(2)}) collective-permute-start(bf16[3,256,512]{2,1,0:T(8,128)(2,1)} %place.8), channel_id=1, source_target_pairs={{0,2},{1,3},{2,4},{3,5},{4,6},{5,7},{6,0},{7,1},{8,10},{9,11},{10,... | collective-permute-start | bytes 2359304 | tf_op jit(solution)/shard_map/ppermute | solution.py:490
  72.2 37.9 %collective-permute-start.4 = (bf16[3,256,512]{2,1,0:T(8,128)(2,1)}, bf16[3,256,512]{2,1,0:T(8,128)(2,1)}, u32[]{:S(2)}, u32[]{:S(2)}) collective-permute-start(bf16[3,256,512]{2,1,0:T(8,128)(2,1)} %place.9), channel_id=1, source_target_pairs={{0,6},{1,7},{2,0},{3,1},{4,2},{5,3},{6,4},{7,5},{8,14},{9,15},{10,... | collective-permute-start | bytes 2359304 | tf_op jit(solution)/shard_map/ppermute | solution.py:490
  76.3 33.7 %collective-permute-start.5 = (bf16[3,256,512]{2,1,0:T(8,128)(2,1)}, bf16[3,256,512]{2,1,0:T(8,128)(2,1)}, u32[]{:S(2)}, u32[]{:S(2)}) collective-permute-start(bf16[3,256,512]{2,1,0:T(8,128)(2,1)} %place.10), channel_id=1, source_target_pairs={{0,1},{1,0},{2,3},{3,2},{4,5},{5,4},{6,7},{7,6},{8,9},{9,8},{10,11... | collective-permute-start | bytes 2359304 | tf_op jit(solution)/shard_map/ppermute | solution.py:490
  94.7 31.6 %collective-permute-start.1 = (bf16[3,256,512]{2,1,0:T(8,128)(2,1)}, bf16[3,256,512]{2,1,0:T(8,128)(2,1)}, u32[]{:S(2)}, u32[]{:S(2)}) collective-permute-start(bf16[3,256,512]{2,1,0:T(8,128)(2,1)} %place.6), channel_id=1, source_target_pairs={{0,3},{1,2},{2,5},{3,4},{4,7},{5,6},{6,1},{7,0},{8,11},{9,10},{10,... | collective-permute-start | bytes 2359304 | tf_op jit(solution)/shard_map/ppermute | solution.py:490
  94.7 31.6 %collective-permute-start.2 = (bf16[3,256,512]{2,1,0:T(8,128)(2,1)}, bf16[3,256,512]{2,1,0:T(8,128)(2,1)}, u32[]{:S(2)}, u32[]{:S(2)}) collective-permute-start(bf16[3,256,512]{2,1,0:T(8,128)(2,1)} %place.7), channel_id=1, source_target_pairs={{0,7},{1,6},{2,1},{3,0},{4,3},{5,2},{6,5},{7,4},{8,15},{9,14},{10,... | collective-permute-start | bytes 2359304 | tf_op jit(solution)/shard_map/ppermute | solution.py:490
